TPU v7x, 32 devices: a whole 2x2x4 slice. The times are simulated.
32 devices in a mesh: fsdp: 4 (over x, core), ctx: 2 (over y), tp: 4 (over z).
Axes of the slice: x: 2, y: 2, z: 4, core: 2. Of those that a mesh axis runs over, the one named last changes fastest.
Arguments:
- tokens: bfloat16 [8, 1024, 768], P('fsdp', 'ctx'), may hold values from -6 to 6
- ln1_gain: float32 [768], replicated, may hold values from 0.1 to 1.9
- ln1_bias: float32 [768], replicated, may hold values from -1.75 to 1.75
- qkv_weight: bfloat16 [3, 768, 768], P(None, 'fsdp', 'tp'), may hold values from -0.21875 to 0.21875
- qv_bias: float32 [2, 768], P(None, 'tp'), may hold values from -1.25 to 1.25
- out_weight: bfloat16 [768, 768], P('tp', 'fsdp'), may hold values from -1.25 to 1.25
- out_bias: float32 [768], replicated, may hold values from -1.75 to 1.75
- ln2_gain: float32 [768], replicated, may hold values from 0.1 to 1.9
- ln2_bias: float32 [768], replicated, may hold values from -1.75 to 1.75
- fc_weight: bfloat16 [768, 3072], P('fsdp', 'tp'), may hold values from -0.21875 to 0.21875
- fc_bias: float32 [3072], P('tp'), may hold values from -3 to 3
- proj_weight: bfloat16 [3072, 768], P('tp', 'fsdp'), may hold values from -0.109375 to 0.109375
- proj_bias: float32 [768], replicated, may hold values from -1.75 to 1.75
- block_order: int32 [4], replicated, may hold values from 0 to 3, as said below
- out_grad: bfloat16 [8, 1024, 768], P('fsdp', 'ctx'), may hold values from -6 to 6
Outputs:
- result: bfloat16 [8, 1024, 768], P('fsdp', 'ctx')
- tokens_grad: float32 [8, 1024, 768], P('fsdp', 'ctx')
- ln1_gain_grad: float32 [768], replicated
- ln1_bias_grad: float32 [768], replicated
- qkv_weight_grad: float32 [3, 768, 768], P(None, 'fsdp', 'tp')
- qv_bias_grad: float32 [2, 768], P(None, 'tp')
- out_weight_grad: float32 [768, 768], P('tp', 'fsdp')
- out_bias_grad: float32 [768], replicated
- ln2_gain_grad: float32 [768], replicated
- ln2_bias_grad: float32 [768], replicated
- fc_weight_grad: float32 [768, 3072], P('fsdp', 'tp')
- fc_bias_grad: float32 [3072], P('tp')
- proj_weight_grad: float32 [3072, 768], P('tp', 'fsdp')
- proj_bias_grad: float32 [768], replicated
Inputs may be any that keep to these rules, and one draw needn't show every extreme that they name: block_order is a permutation of the 4 block numbers.
All inputs are finite; a program needn't handle non-finite values.
Results may differ from a plain program's by a relative error of at most 0.0099.
Values may be sent and summed in bfloat16 or wider, within the bound.
A program may use at most 192 MiB of HBM per device.

v0:
```python
import jax
import jax.numpy as jnp
from jax import lax
from jax.sharding import PartitionSpec as P

HD = 64


def gelu_curve(values):
    return jax.nn.gelu(values, approximate=True)


def normalized(values):
    centre = jnp.mean(values, axis=-1, keepdims=True)
    centred = values - centre
    scale = lax.rsqrt(jnp.mean(centred * centred, axis=-1, keepdims=True) + 1e-05)
    return (centred * scale, scale)


def norm_back(grad_in, gain, normed, scale):
    scaled = grad_in * gain
    return scale * (
        scaled
        - jnp.mean(scaled, axis=-1, keepdims=True)
        - normed * jnp.mean(scaled * normed, axis=-1, keepdims=True)
    )


def query_side(query_rows, pair_rows, grad_rows, lse_rows, visible):
    columns = query_rows.shape[1]
    heads_here = columns // HD
    length = pair_rows.shape[0]
    query_grad = jnp.zeros(query_rows.shape, jnp.float32)
    delta_cols = jnp.zeros((query_rows.shape[0], heads_here), jnp.float32)
    pair_term = jnp.zeros((length, 2 * columns), jnp.float32)

    def one_head(head_index, running):
        query_grad, pair_term, delta_cols = running
        start = head_index * HD
        query_head = lax.dynamic_slice_in_dim(query_rows, start, HD, 1)
        key_head = lax.dynamic_slice_in_dim(pair_rows, start, HD, 1)
        value_head = lax.dynamic_slice_in_dim(pair_rows, columns + start, HD, 1)
        grad_head = lax.dynamic_slice_in_dim(grad_rows, start, HD, 1)
        lse_head = lax.dynamic_slice_in_dim(lse_rows, head_index, 1, 1)
        scores = (
            jnp.einsum("qd,kd->qk", query_head, key_head, preferred_element_type=jnp.float32)
            * 0.125
        )
        scores = jnp.where(visible, scores, -1e30)
        prob_rows = jnp.exp(scores - lse_head)
        prob_grad = jnp.einsum(
            "qd,kd->qk", grad_head, value_head, preferred_element_type=jnp.float32
        )
        row_delta = jnp.sum(prob_rows * prob_grad, axis=-1, keepdims=True)
        score_grad = (prob_rows * (prob_grad - row_delta)).astype(jnp.bfloat16)
        query_part = (
            jnp.einsum("qk,kd->qd", score_grad, key_head, preferred_element_type=jnp.float32)
            * 0.125
        )
        query_grad = lax.dynamic_update_slice_in_dim(query_grad, query_part, start, 1)
        delta_cols = lax.dynamic_update_slice_in_dim(delta_cols, row_delta, head_index, 1)
        key_part = (
            jnp.einsum("qk,qd->kd", score_grad, query_head, preferred_element_type=jnp.float32)
            * 0.125
        )
        value_part = jnp.einsum(
            "qk,qd->kd",
            prob_rows.astype(jnp.bfloat16),
            grad_head,
            preferred_element_type=jnp.float32,
        )
        pair_term = lax.dynamic_update_slice_in_dim(pair_term, key_part, start, 1)
        pair_term = lax.dynamic_update_slice_in_dim(pair_term, value_part, columns + start, 1)
        return (query_grad, pair_term, delta_cols)

    return lax.fori_loop(0, heads_here, one_head, (query_grad, pair_term, delta_cols))


def body(
    tokens,
    ln1_gain,
    ln1_bias,
    qkv_weight,
    qv_bias,
    out_weight,
    out_bias,
    ln2_gain,
    ln2_bias,
    fc_weight,
    fc_bias,
    proj_weight,
    proj_bias,
    block_order,
    out_grad,
):
    seq_count, seq_rows, model_width = tokens.shape
    ctx_count = lax.axis_size("ctx")
    length = seq_rows * ctx_count
    block_rows = length // (2 * ctx_count)
    all_rows = jnp.arange(length, dtype=jnp.int32)
    slot_ids = jnp.arange(2 * ctx_count, dtype=jnp.int32)
    owner = all_rows[:, None] // block_rows == slot_ids[None, :]
    place_all = (
        jnp.sum(jnp.where(owner, block_order[None, :], 0), axis=1) * block_rows
        + all_rows % block_rows
    )
    place_here = lax.dynamic_slice_in_dim(place_all, lax.axis_index("ctx") * seq_rows, seq_rows)
    visible = place_here[:, None] >= place_all[None, :]
    whole_qkv, whole_out, whole_fc, whole_proj = (
        lax.all_gather(qkv_weight, "fsdp", axis=1, tiled=True),
        lax.all_gather(out_weight, "fsdp", axis=1, tiled=True),
        lax.all_gather(fc_weight, "fsdp", axis=0, tiled=True),
        lax.all_gather(proj_weight, "fsdp", axis=1, tiled=True),
    )
    columns = whole_qkv.shape[-1]
    heads_here = columns // HD
    total_rows = seq_count * seq_rows
    inputs = tokens.reshape(total_rows, model_width).astype(jnp.float32)
    normed_one, scale_one = normalized(inputs)
    act_one = (normed_one * ln1_gain + ln1_bias).astype(jnp.bfloat16)
    proj_qkv = jnp.einsum("td,cdh->cth", act_one, whole_qkv, preferred_element_type=jnp.float32)
    query = (proj_qkv[0] + qv_bias[0]).astype(jnp.bfloat16)
    key = proj_qkv[1].astype(jnp.bfloat16)
    value = (proj_qkv[2] + qv_bias[1]).astype(jnp.bfloat16)
    key_value = jnp.concatenate([key, value], axis=1).reshape(seq_count, seq_rows, 2 * columns)
    pair_whole = lax.all_gather(key_value, "ctx", axis=1, tiled=True)
    query_three = query.reshape(seq_count, seq_rows, columns)
    anchor = jnp.zeros((), jnp.int32)

    def forward_item(counter, running):
        attended, log_sums = running
        sequence = counter // heads_here
        head_index = counter % heads_here
        query_head = lax.dynamic_slice(
            query_three, (sequence, anchor, head_index * HD), (1, seq_rows, HD)
        )[0]
        key_head = lax.dynamic_slice(
            pair_whole, (sequence, anchor, head_index * HD), (1, length, HD)
        )[0]
        value_head = lax.dynamic_slice(
            pair_whole, (sequence, anchor, columns + head_index * HD), (1, length, HD)
        )[0]
        scores = (
            jnp.einsum("qd,kd->qk", query_head, key_head, preferred_element_type=jnp.float32)
            * 0.125
        )
        scores = jnp.where(visible, scores, -1e30)
        row_top = jnp.max(scores, axis=-1, keepdims=True)
        weights = jnp.exp(scores - row_top)
        row_total = jnp.sum(weights, axis=-1, keepdims=True)
        prob_low = (weights / row_total).astype(jnp.bfloat16)
        out_head = jnp.einsum("qk,kd->qd", prob_low, value_head, preferred_element_type=jnp.float32)
        attended = lax.dynamic_update_slice(
            attended, out_head[None], (sequence, anchor, head_index * HD)
        )
        log_sums = lax.dynamic_update_slice(
            log_sums, (row_top + jnp.log(row_total))[None], (sequence, anchor, head_index)
        )
        return (attended, log_sums)

    attended, log_sums = lax.fori_loop(
        0,
        seq_count * heads_here,
        forward_item,
        (
            jnp.zeros((seq_count, seq_rows, columns), jnp.float32),
            jnp.zeros((seq_count, seq_rows, heads_here), jnp.float32),
        ),
    )
    mixed = attended.reshape(total_rows, columns).astype(jnp.bfloat16)
    attn_out = (
        lax.psum(jnp.dot(mixed, whole_out, preferred_element_type=jnp.float32), "tp") + out_bias
    )
    middle = inputs + attn_out
    normed_two, scale_two = normalized(middle)
    act_two = (normed_two * ln2_gain + ln2_bias).astype(jnp.bfloat16)
    hidden_pre = jnp.dot(act_two, whole_fc, preferred_element_type=jnp.float32) + fc_bias
    hidden_out, gelu_back = jax.vjp(gelu_curve, hidden_pre)
    hidden = hidden_out.astype(jnp.bfloat16)
    branch = (
        lax.psum(
            jnp.dot(hidden, whole_proj, preferred_element_type=jnp.float32).astype(jnp.bfloat16),
            "tp",
        ).astype(jnp.float32)
        + proj_bias
    )
    result = (middle + branch).astype(jnp.bfloat16).reshape(seq_count, seq_rows, model_width)
    upstream_low = out_grad.reshape(total_rows, model_width)
    upstream = upstream_low.astype(jnp.float32)
    proj_bias_grad = jnp.sum(upstream, axis=0)
    proj_grad = jnp.einsum("tf,td->fd", hidden, upstream_low, preferred_element_type=jnp.float32)
    hidden_grad = jnp.einsum(
        "td,fd->tf", upstream_low, whole_proj, preferred_element_type=jnp.float32
    )
    pre_grad = gelu_back(hidden_grad)[0].astype(jnp.bfloat16)
    fc_bias_grad = jnp.sum(pre_grad.astype(jnp.float32), axis=0)
    fc_grad = jnp.einsum("td,tf->df", act_two, pre_grad, preferred_element_type=jnp.float32)
    act_two_grad = lax.psum(
        jnp.einsum("tf,df->td", pre_grad, whole_fc, preferred_element_type=jnp.float32), "tp"
    )
    ln2_gain_grad = jnp.sum(act_two_grad * normed_two, axis=0)
    ln2_bias_grad = jnp.sum(act_two_grad, axis=0)
    middle_grad = upstream + norm_back(act_two_grad, ln2_gain, normed_two, scale_two)
    attn_grad = middle_grad.astype(jnp.bfloat16)
    out_bias_grad = jnp.sum(attn_grad.astype(jnp.float32), axis=0)
    out_grad_weight = jnp.einsum("th,td->hd", mixed, attn_grad, preferred_element_type=jnp.float32)
    mixed_grad = (
        jnp.einsum("td,hd->th", attn_grad, whole_out, preferred_element_type=jnp.float32)
        .astype(jnp.bfloat16)
        .reshape(seq_count, seq_rows, columns)
    )
    query_grads = []
    pair_grads = []
    for sequence in range(seq_count):
        query_grad, pair_term, delta_cols = query_side(
            query_three[sequence],
            pair_whole[sequence],
            mixed_grad[sequence],
            log_sums[sequence],
            visible,
        )
        pair_grad = lax.psum_scatter(pair_term, "ctx", scatter_dimension=0, tiled=True)
        query_grads.append(query_grad)
        pair_grads.append(pair_grad)
    query_grad_low = jnp.concatenate(query_grads, axis=0).astype(jnp.bfloat16)
    pair_low = jnp.concatenate(pair_grads, axis=0).astype(jnp.bfloat16)
    stacked = jnp.stack([query_grad_low, pair_low[:, :columns], pair_low[:, columns:]])
    qv_bias_grad = jnp.stack(
        [
            jnp.sum(stacked[0].astype(jnp.float32), axis=0),
            jnp.sum(stacked[2].astype(jnp.float32), axis=0),
        ]
    )
    qkv_grad = jnp.einsum("td,cth->cdh", act_one, stacked, preferred_element_type=jnp.float32)
    act_one_grad = lax.psum(
        jnp.einsum("cth,cdh->td", stacked, whole_qkv, preferred_element_type=jnp.float32), "tp"
    )
    ln1_gain_grad = jnp.sum(act_one_grad * normed_one, axis=0)
    ln1_bias_grad = jnp.sum(act_one_grad, axis=0)
    tokens_grad = (middle_grad + norm_back(act_one_grad, ln1_gain, normed_one, scale_one)).reshape(
        seq_count, seq_rows, model_width
    )
    shard_qkv, shard_out, shard_fc, shard_proj = (
        lax.psum_scatter(qkv_grad, "fsdp", scatter_dimension=1, tiled=True),
        lax.psum_scatter(out_grad_weight, "fsdp", scatter_dimension=1, tiled=True),
        lax.psum_scatter(fc_grad, "fsdp", scatter_dimension=0, tiled=True),
        lax.psum_scatter(proj_grad, "fsdp", scatter_dimension=1, tiled=True),
    )
    shard_qkv, shard_out, shard_fc, shard_proj = lax.psum(
        (shard_qkv, shard_out, shard_fc, shard_proj), "ctx"
    )
    small_sums = lax.psum(
        (
            ln1_gain_grad,
            ln1_bias_grad,
            qv_bias_grad,
            out_bias_grad,
            ln2_gain_grad,
            ln2_bias_grad,
            fc_bias_grad,
            proj_bias_grad,
        ),
        ("fsdp", "ctx"),
    )
    return (
        result,
        tokens_grad,
        small_sums[0],
        small_sums[1],
        shard_qkv,
        small_sums[2],
        shard_out,
        small_sums[3],
        small_sums[4],
        small_sums[5],
        shard_fc,
        small_sums[6],
        shard_proj,
        small_sums[7],
    )


def solution(mesh):
    in_specs = (
        P("fsdp", "ctx", None),
        P(),
        P(),
        P(None, "fsdp", "tp"),
        P(None, "tp"),
        P("tp", "fsdp"),
        P(),
        P(),
        P(),
        P("fsdp", "tp"),
        P("tp"),
        P("tp", "fsdp"),
        P(),
        P(),
        P("fsdp", "ctx", None),
    )
    out_specs = (
        P("fsdp", "ctx", None),
        P("fsdp", "ctx", None),
        P(),
        P(),
        P(None, "fsdp", "tp"),
        P(None, "tp"),
        P("tp", "fsdp"),
        P(),
        P(),
        P(),
        P("fsdp", "tp"),
        P("tp"),
        P("tp", "fsdp"),
        P(),
    )
    return jax.shard_map(body, mesh=mesh, in_specs=in_specs, out_specs=out_specs, check_vma=False)
```

profile of v0, /device:TPU:0, one launch (start us, length us, event | category | flops | bytes accessed | tf_op | source)
XLA Modules:
  0.0 816.9 jit_solution(1400386524486620718)
XLA Ops:
  8.1 1.8 convert_reduce_fusion
  10.9 14.3 %all_gather.15 = bf16[3,768,192]{2,0,1:T(4,128)(2,1)S(1)} all-gather(bf16[3,192,192]{2,0,1:T(4,128)(2,1)S(1)} %copy.100), channel_id=1, replica_groups=mesh['fsdp'=4,'ctx'=2,'tp'=4] {'fsdp'}, dimensions={1}, use_global_device_ids=true | all-gather | bytes 1105920 | tf_op jit(solution)/shard_map/all_gather | solution.py:110
  25.2 2.0 copy.101
  29.6 1.4 copy-done.13
  34.7 6.6 all_gather.17
  41.3 20.8 %all-gather.4.cloned.1.call-done = bf16[2,1024,384]{1,2,0:T(8,128)(2,1)} async-done(((bf16[2,512,384]{1,2,0:T(8,128)(2,1)}), bf16[2,1024,384]{1,2,0:T(8,128)(2,1)}) %all-gather.4.cloned.1.call-update) | async-done | bytes 1572880 | tf_op jit(solution)/shard_map/all_gather | solution.py:126
  62.1 1.9 copy.105
  64.1 12.1 %while.54 = (s32[]{:T(128)}, bf16[2,512,192]{1,2,0:T(8,128)(2,1)S(1)}, f32[2,512,3]{1,2,0:T(4,128)S(1)}, bf16[2,512,192]{2,1,0:T(8,128)(2,1)S(1)}, bf16[2,1024,3...) while((s32[]{:T(128)}, ...), condition=%wide.region_6.7_spmd.clone, body=%wide.region_3.6_spmd.clone.sunk | while | flops 138935840 | bytes 7109057 | solution.py:161
  77.0 2.3 fusion.101
  80.7 119.8 %all-reduce.8.cloned.1.call-done = f32[1024,768]{1,0:T(8,128)} async-done(((f32[1024,768]{1,0:T(8,128)}), f32[1024,768]{1,0:T(8,128)}) %all-reduce.8.cloned.1.call-update) | async-done | bytes 3145744 | tf_op jit(solution)/shard_map/psum | solution.py:172
  200.5 2.8 fusion.94
  204.0 1.7 add_convert_fusion.1
  205.8 4.8 fusion.102
  210.6 6.4 convert_reduce_fusion.2
  217.0 1.2 copy-done.55
  218.1 3.1 fusion.103
  221.3 5.5 convolution_convert_fusion
  227.1 1.4 fusion.74
  228.7 1.3 slice_bitcast_fusion.1
  230.0 2.3 copy.110
  232.3 2.3 copy.114
  234.6 1.3 slice_bitcast_fusion.3
  236.0 105.5 %all-reduce.12.cloned.1.call-done = f32[1024,768]{1,0:T(8,128)} async-done(((f32[1024,768]{1,0:T(8,128)}), f32[1024,768]{1,0:T(8,128)}) %all-reduce.12.cloned.1.call-update) | async-done | bytes 3145744 | tf_op jit(solution)/shard_map/psum | solution.py:198
  341.5 3.7 multiply_reduce_fusion.2
  345.8 66.5 %all-reduce.10.cloned.1.call-done = bf16[1024,768]{1,0:T(8,128)(2,1)} async-done(((bf16[1024,768]{1,0:T(8,128)(2,1)}), bf16[1024,768]{1,0:T(8,128)(2,1)}) %all-reduce.10.cloned.1.call-update) | async-done | bytes 1572880 | tf_op jit(solution)/shard_map/psum | solution.py:181
  412.3 5.2 convert_reduce_fusion.3
  419.5 11.1 %while.55 = (s32[]{:T(128)}, bf16[512,192]{0,1:T(8,128)(2,1)S(1)}, f32[1024,384]{0,1:T(8,128)S(1)}, bf16[512,192]{0,1:T(8,128)(2,1)S(1)}, bf16[1024,384]{1,0:T(8...) while((s32[]{:T(128)}, bf16[512,192]{0,1:T(8,128)(2,1)S(1)}, ...), condition=%wide.region_16.17_spmd.clone, body=%wide.region_14.16_spmd.clone.sunk | while | flops 340884992 | bytes 17449256 | solution.py:76
  430.6 1.1 copy-done.6
  432.5 1.4 broadcast.259.clone.1
  433.9 26.1 %while.56 = (s32[]{:T(128)}, bf16[512,192]{0,1:T(8,128)(2,1)}, f32[1024,384]{0,1:T(8,128)}, bf16[512,192]{0,1:T(8,128)(2,1)S(1)}, bf16[1024,384]{1,0:T(8,128)(2,...) while((s32[]{:T(128)}, bf16[512,192]{0,1:T(8,128)(2,1)}, ...), condition=%wide.region_19.20_spmd.clone, body=%wide.region_17.19_spmd.clone.sunk | while | flops 340884992 | bytes 19022176 | solution.py:76
  434.8 1.6 fusion.175
  436.3 2.0 multiply_reduce_fusion.10
  439.3 1.5 fusion.176
  443.5 1.5 fusion.175
  445.0 2.0 multiply_reduce_fusion.10
  447.9 1.5 fusion.176
  452.1 1.5 fusion.175
  453.6 2.0 multiply_reduce_fusion.10
  456.5 1.5 fusion.176
  460.1 2.6 convolution_bitcast_fusion.2
  462.8 1.3 convert.23
  464.1 21.4 %reduce-scatter.13.cloned.1.call-done = f32[512,384]{0,1:T(8,128)} async-done(((f32[1024,384]{0,1:T(8,128)}), f32[512,384]{0,1:T(8,128)}) %reduce-scatter.13.cloned.1.call-update) | async-done | bytes 786448 | tf_op jit(solution)/shard_map/reduce_scatter | solution.py:222
  485.5 1.2 convert.24
  488.5 2.3 fusion.71
  490.8 3.0 copy.119
  493.8 2.8 reshape.261
  496.9 5.8 fusion.92
  502.8 1.3 copy-done.16
  504.1 2.9 fusion.104
  508.5 3.1 convolution_bitcast_fusion.1
  511.7 1.7 copy.122
  513.5 30.8 %reduce-scatter.19.cloned.1.call-done = f32[192,576]{1,0:T(8,128)} async-done(((f32[768,576]{1,0:T(8,128)}), f32[192,576]{1,0:T(8,128)}) %reduce-scatter.19.cloned.1.call-update) | async-done | bytes 442384
  544.3 1.4 reshape.262
  546.7 32.9 %reduce-scatter.17.cloned.1.call-done = f32[768,192]{0,1:T(8,128)} async-done(((f32[768,768]{0,1:T(8,128)}), f32[768,192]{0,1:T(8,128)}) %reduce-scatter.17.cloned.1.call-update) | async-done | bytes 589840 | tf_op jit(solution)/shard_map/reduce_scatter | solution.py:247
  579.7 35.2 %reduce-scatter.15.cloned.1.call-done = f32[192,768]{1,0:T(8,128)} async-done(((f32[768,768]{1,0:T(8,128)}), f32[192,768]{1,0:T(8,128)}) %reduce-scatter.15.cloned.1.call-update) | async-done | bytes 589840 | tf_op jit(solution)/shard_map/reduce_scatter | solution.py:246
  615.8 1.2 convert_reduce_fusion.5
  618.1 120.8 %all-reduce.14.cloned.1.call-done = f32[1024,768]{1,0:T(8,128)} async-done(((f32[1024,768]{1,0:T(8,128)}), f32[1024,768]{1,0:T(8,128)}) %all-reduce.14.cloned.1.call-update) | async-done | bytes 3145744 | tf_op jit(solution)/shard_map/psum | solution.py:235
  738.9 3.1 fusion.68
  742.0 25.4 %all-reduce = (f32[768]{0:T(1024)}, f32[768]{0:T(1024)}, f32[2,192]{1,0:T(2,128)}, f32[768]{0:T(1024)}, f32[768]{0:T(1024)}, /*index=5*/f32[768]{0:T(1024)}, f32[768]{0:T(1024)}, f32[768]{0:T(1024)}) all-reduce(f32[768]{0:T(1024)S(1)} %get-tuple-element.847, ...), channel_id=1, replica_groups=mesh['fsdp'=4,'ctx'=2,'tp'=4] {'fsdp','ctx'}, use_global_device_ids=true, to_apply=%region_26.27 | all-reduce | flops 5760 | bytes 46080 | tf_op jit(solution)/shard_map/psum | solution.py:252
  767.5 4.5 fusion.67
  772.0 30.4 %all-reduce.16.cloned.1.call-done = (f32[3,192,192]{1,2,0:T(8,128)}, f32[192,192]{1,0:T(8,128)}, f32[192,768]{1,0:T(8,128)}, f32[768,192]{0,1:T(8,128)}) async-done(((f32[3,192,192]{1,2,0:T(8,128)}, f32[192,192]{1,0:T(8,128)}, f32[192,768]{1,0:T(8,128)}, f32[768,192]{0,1:T(8,128)}), (f32[3,192,192]{1,2,0:T(8,128)}, f32[192,192]{1,0:T(8,128)}, f32[192,768]{1,0:T(8,128)}, ...) | async-done | bytes 1769488 | tf_op jit(solution)/shard_map/psum | solution.py:249
  802.4 2.2 copy.117
  804.6 1.6 copy.195
  806.2 1.9 copy.196
  (257 shorter events, 55.1 us)
Async XLA Ops:
  8.0 1.9 copy-start
  8.0 2.5 copy-start.31
  8.0 54.1 %all-gather.4.cloned.1.call-start = ((), (), s32[]{:S(2)}) async-start(), calls=%async_computation.6 | async-start | bytes 2359296 | tf_op jit(solution)/shard_map/all_gather | solution.py:126
  10.6 16.7 %copy-start.33 = (f32[1,4,2,128]{3,1,2,0:T(4,128)}, f32[1,4,2,128]{3,1,2,0:T(4,128)S(1)}, u32[]{:S(2)}) copy-start(f32[1,4,2,128]{3,1,2,0:T(4,128)S(1)} %copy.148) | copy-start | bytes 12292
  10.8 16.4 %copy-start.37 = (f32[768]{0:T(1024)S(1)}, f32[768]{0:T(1024)}, u32[]{:S(2)}) copy-start(f32[768]{0:T(1024)} %param.22) | copy-start | bytes 9220
  10.8 16.4 %copy-start.46 = (f32[768]{0:T(1024)S(1)}, f32[768]{0:T(1024)}, u32[]{:S(2)}) copy-start(f32[768]{0:T(1024)} %param.23) | copy-start | bytes 9220
  27.2 1.2 copy-start.17
  27.9 1.6 copy-start.14
  29.5 1.5 copy-start.13
  29.5 1.6 copy-start.50
  32.1 1.9 copy-start.32
  33.0 1.5 copy-start.51
  33.0 8.2 %copy-start.44 = (f32[1,192]{1,0:T(1,128)S(1)}, f32[1,192]{1,0:T(1,128)}, u32[]{:S(2)}) copy-start(f32[1,192]{1,0:T(1,128)} %get-tuple-element.943) | copy-start | bytes 2308
  34.0 166.5 %all-reduce.8.cloned.1.call-start = ((), (), s32[]{:S(2)}) async-start(), calls=%async_computation.7 | async-start | bytes 6291456 | tf_op jit(solution)/shard_map/psum | solution.py:172
  41.2 35.0 %copy-start.11 = (bf16[192,768]{0,1:T(8,128)(2,1)}, bf16[192,768]{0,1:T(8,128)(2,1)S(1)}, u32[]{:S(2)}) copy-start(bf16[192,768]{0,1:T(8,128)(2,1)S(1)} %all_gather.17) | copy-start | bytes 884740
  76.2 3.1 copy-start.35
  79.3 121.2 %copy-start.47 = (f32[768]{0:T(1024)S(1)}, f32[768]{0:T(1024)}, u32[]{:S(2)}) copy-start(f32[768]{0:T(1024)} %param.27) | copy-start | bytes 9220
  79.3 126.5 %all-gather.6.cloned.1.call-start = ((), (), s32[]{:S(2)}) async-start(), calls=%async_computation.8 | async-start | bytes 1474560 | tf_op jit(solution)/shard_map/all_gather | solution.py:112
  79.9 130.7 %all-gather.8.cloned.1.call-start = ((), (), s32[]{:S(2)}) async-start(), calls=%async_computation.9 | async-start | bytes 1474560 | tf_op jit(solution)/shard_map/all_gather | solution.py:113
  80.5 261.0 %all-reduce.12.cloned.1.call-start = ((), (), s32[]{:S(2)}) async-start(), calls=%async_computation.11 | async-start | bytes 6291456 | tf_op jit(solution)/shard_map/psum | solution.py:198
  204.0 1.7 copy-start.36
  205.8 4.8 copy-start.53
  210.6 7.6 copy-start.52
  221.3 191.0 %all-reduce.10.cloned.1.call-start = ((), (), s32[]{:S(2)}) async-start(), calls=%async_computation.10 | async-start | bytes 3145728 | tf_op jit(solution)/shard_map/psum | solution.py:181
  221.3 5.8 copy-start.45
  226.8 236.0 %reduce-scatter.11.cloned.1.call-start = ((), (), s32[]{:S(2)}) async-start(), calls=%async_computation.12 | async-start | bytes 2359296 | tf_op jit(solution)/shard_map/reduce_scatter | solution.py:222
  227.1 1.6 copy-start.5
  412.3 5.2 copy-start.12
  417.5 1.7 copy-start.2
  417.5 1.9 copy-start.4
  430.6 3.3 copy-start.23
  430.6 3.3 copy-start.8
  431.8 53.8 %reduce-scatter.13.cloned.1.call-start = ((), (), s32[]{:S(2)}) async-start(), calls=%async_computation.13 | async-start | bytes 2359296 | tf_op jit(solution)/shard_map/reduce_scatter | solution.py:222
  433.9 26.2 %copy-start.3 = (f32[1024,768]{1,0:T(8,128)S(1)}, f32[1024,768]{1,0:T(8,128)}, u32[]{:S(2)}) copy-start(f32[1024,768]{1,0:T(8,128)} %copy-done.2) | copy-start | bytes 9437188
  440.8 2.1 copy-start.20
  449.4 2.0 copy-start.20
  458.0 2.0 copy-start.20
  460.0 51.7 %reduce-scatter.21.cloned.1.call-start = ((), (), s32[]{:S(2)}) async-start(), calls=%async_computation.18 | async-start | bytes 983040
  462.7 25.7 %copy-start.15 = (bf16[1024,768]{1,0:T(8,128)(2,1)S(1)}, bf16[1024,768]{1,0:T(8,128)(2,1)}, u32[]{:S(2)}) copy-start(bf16[1024,768]{1,0:T(8,128)(2,1)} %copy-done.14) | copy-start | bytes 4718596
  462.7 25.7 %copy-start.21 = (bf16[512,192]{0,1:T(8,128)(2,1)S(1)}, bf16[512,192]{0,1:T(8,128)(2,1)}, u32[]{:S(2)}) copy-start(bf16[512,192]{0,1:T(8,128)(2,1)} %get-tuple-element.574) | copy-start | bytes 589828
  462.7 25.7 %copy-start.24 = (bf16[512,192]{0,1:T(8,128)(2,1)S(1)}, bf16[512,192]{0,1:T(8,128)(2,1)}, u32[]{:S(2)}) copy-start(bf16[512,192]{0,1:T(8,128)(2,1)} %copy-done.23) | copy-start | bytes 589828
  462.8 81.5 %reduce-scatter.19.cloned.1.call-start = ((), (), s32[]{:S(2)}) async-start(), calls=%async_computation.17 | async-start | bytes 2457600
  493.8 3.1 copy-start.54
  496.6 83.0 %reduce-scatter.17.cloned.1.call-start = ((), (), s32[]{:S(2)}) async-start(), calls=%async_computation.16 | async-start | bytes 2949120 | tf_op jit(solution)/shard_map/reduce_scatter | solution.py:247
  496.9 5.9 copy-start.56
  502.7 1.4 copy-start.16
  502.7 112.1 %reduce-scatter.15.cloned.1.call-start = ((), (), s32[]{:S(2)}) async-start(), calls=%async_computation.15 | async-start | bytes 2949120 | tf_op jit(solution)/shard_map/reduce_scatter | solution.py:246
  507.0 1.2 copy-start.18
  507.0 1.2 copy-start.22
  507.0 1.2 copy-start.25
  507.0 1.4 copy-start.28
  507.1 1.5 copy-start.30
  507.1 231.8 %all-reduce.14.cloned.1.call-start = ((), (), s32[]{:S(2)}) async-start(), calls=%async_computation.14 | async-start | bytes 6291456 | tf_op jit(solution)/shard_map/psum | solution.py:235
  511.7 290.8 %all-reduce.16.cloned.1.call-start = ((), (), s32[]{:S(2)}) async-start(), calls=%async_computation.19 | async-start | bytes 3932160 | tf_op jit(solution)/shard_map/psum | solution.py:249
  513.5 101.5 %copy-start.7 = (bf16[2,512,768]{2,1,0:T(8,128)(2,1)S(1)}, bf16[2,512,768]{2,1,0:T(8,128)(2,1)}, u32[]{:S(2)}) copy-start(bf16[2,512,768]{2,1,0:T(8,128)(2,1)} %param.35) | copy-start | bytes 4718596
  614.9 124.0 %copy-start.1 = (bf16[2,512,768]{2,1,0:T(8,128)(2,1)S(1)}, bf16[2,512,768]{2,1,0:T(8,128)(2,1)}, u32[]{:S(2)}) copy-start(bf16[2,512,768]{2,1,0:T(8,128)(2,1)} %param.21) | copy-start | bytes 4718596
  614.9 124.0 %copy-start.34 = (f32[1,4,2,128]{3,1,2,0:T(4,128)S(1)}, f32[1,4,2,128]{3,1,2,0:T(4,128)}, u32[]{:S(2)}) copy-start(f32[1,4,2,128]{3,1,2,0:T(4,128)} %copy-done.33) | copy-start | bytes 12292
  614.9 124.0 %copy-start.38 = (f32[768]{0:T(1024)S(1)}, f32[768]{0:T(1024)}, u32[]{:S(2)}) copy-start(f32[768]{0:T(1024)} %param.22) | copy-start | bytes 9220
  618.0 124.0 %copy-start.40 = (f32[768]{0:T(1024)S(1)}, f32[768]{0:T(1024)}, u32[]{:S(2)}) copy-start(f32[768]{0:T(1024)} %get-tuple-element.917) | copy-start | bytes 9220
  618.0 123.9 %copy-start.41 = (f32[768]{0:T(1024)S(1)}, f32[768]{0:T(1024)}, u32[]{:S(2)}) copy-start(f32[768]{0:T(1024)} %convert_reduce_fusion.1) | copy-start | bytes 9220
  618.1 123.9 %copy-start.42 = (f32[768]{0:T(1024)S(1)}, f32[768]{0:T(1024)}, u32[]{:S(2)}) copy-start(f32[768]{0:T(1024)} %get-tuple-element.845) | copy-start | bytes 9220
  618.1 123.9 %copy-start.43 = (f32[768]{0:T(1024)S(1)}, f32[768]{0:T(1024)}, u32[]{:S(2)}) copy-start(f32[768]{0:T(1024)} %get-tuple-element.851) | copy-start | bytes 9220
  618.1 123.9 %copy-start.49 = (f32[768]{0:T(1024)S(1)}, f32[768]{0:T(1024)}, u32[]{:S(2)}) copy-start(f32[768]{0:T(1024)} %get-tuple-element.915) | copy-start | bytes 9220
  802.4 5.7 copy-start.26
  (11 other events, 9.6 us)
Sparse Core Ops, SparseCore 0:
  34.1 28.0 all-gather.3
  79.4 121.0 all-reduce.7
  221.4 120.0 all-reduce.11
  344.3 67.9 all-reduce.9
  431.9 25.2 reduce-scatter.10
  460.2 25.3 reduce-scatter.12
  488.1 23.1 reduce-scatter.20
  513.9 30.3 reduce-scatter.18
  546.8 32.8 reduce-scatter.16
  582.0 32.8 reduce-scatter.14
  617.8 121.0 all-reduce.13
  742.4 60.0 all-reduce.15
Sparse Core Ops, SparseCore 1:
  81.3 17.3 all-gather.5
  100.1 17.3 all-gather.7
where the time goes:
time: 824 us; the launch traced here: 817 us
  waiting for transfers between devices  586 us (71%)
  matrix products  77.9 us (9%)
  local copies, waits for them, and re-layouts  50.1 us (6%)
  blocking collectives  46.3 us (6%)
  other arithmetic  38.2 us (5%)
  between operations  16.8 us (2%)
    psum x1, waiting for transfers between devices, body(): lax.psum(jnp.einsum('cth,cdh->td', stacked, whole_qkv, preferred_element_...  121 us
    psum x1, waiting for transfers between devices, body(): lax.psum(jnp.dot(mixed, whole_out, preferred_element_type=jnp.float32), '...  120 us
    psum x1, waiting for transfers between devices, body(): lax.psum(jnp.einsum('tf,df->td', pre_grad, whole_fc, preferred_element_ty...  106 us
    psum x1, waiting for transfers between devices, body(): lax.psum(jnp.dot(hidden, whole_proj, preferred_element_type=jnp.float32)....  66.5 us
    reduce_scatter x1, waiting for transfers between devices, body(): lax.psum_scatter(fc_grad, 'fsdp', scatter_dimension=0, tiled=True)  35.2 us
    unnamed x126, local copies, waits for them, and re-layouts  33.5 us
    reduce_scatter x1, waiting for transfers between devices, body(): lax.psum_scatter(proj_grad, 'fsdp', scatter_dimension=1, tiled=True)  32.9 us
    unnamed x16, waiting for transfers between devices  32.1 us
  transfers between devices with their start and end apart: 14, of which 10 were waited for; matrix products, arithmetic and copies ran while one was open for 12% of the time, Pallas kernels for 0%

commit v1 on v0

--- a/solution.py
+++ b/solution.py
@@ -24,6 +24,42 @@
         - jnp.mean(scaled, axis=-1, keepdims=True)
         - normed * jnp.mean(scaled * normed, axis=-1, keepdims=True)
     )
+
+
+def swap(values, axis_name, bit):
+    count = lax.axis_size(axis_name)
+    return lax.ppermute(values, axis_name, [(i, i ^ bit) for i in range(count)])
+
+
+def sum_all(values, axis_name):
+    bit = 1
+    while bit < lax.axis_size(axis_name):
+        values = values + swap(values, axis_name, bit)
+        bit *= 2
+    return values
+
+
+def scatter_rows(values, axis_name):
+    count = lax.axis_size(axis_name)
+    index = lax.axis_index(axis_name)
+    lead, rows, width = values.shape
+    values = values.reshape(lead, count, rows // count, width)
+    bit = 1
+    while bit < count:
+        low = (index // bit) % 2
+        pairs = values.reshape(lead, values.shape[1] // 2, 2, rows // count, width)
+        kept = lax.dynamic_index_in_dim(pairs, low, 2, False)
+        given = lax.dynamic_index_in_dim(pairs, 1 - low, 2, False).astype(jnp.bfloat16)
+        values = kept + swap(given, axis_name, bit).astype(jnp.float32)
+        bit *= 2
+    return values[:, 0]
+
+
+def combine(values):
+    low = values.astype(jnp.bfloat16)
+    if lax.axis_size("ctx") == 2:
+        return low.astype(jnp.float32) + swap(low, "ctx", 1).astype(jnp.float32)
+    return lax.psum(low, "ctx").astype(jnp.float32)
 
 
 def query_side(query_rows, pair_rows, grad_rows, lse_rows, visible):
@@ -106,12 +142,11 @@
     )
     place_here = lax.dynamic_slice_in_dim(place_all, lax.axis_index("ctx") * seq_rows, seq_rows)
     visible = place_here[:, None] >= place_all[None, :]
-    whole_qkv, whole_out, whole_fc, whole_proj = (
-        lax.all_gather(qkv_weight, "fsdp", axis=1, tiled=True),
-        lax.all_gather(out_weight, "fsdp", axis=1, tiled=True),
-        lax.all_gather(fc_weight, "fsdp", axis=0, tiled=True),
-        lax.all_gather(proj_weight, "fsdp", axis=1, tiled=True),
-    )
+    whole_qkv = lax.all_gather(qkv_weight, "fsdp", axis=1, tiled=True)
+    whole_out = lax.all_gather(out_weight.T, "fsdp", axis=0, tiled=True).T
+    all_out = lax.all_gather(whole_out, "tp", axis=0, tiled=True)
+    whole_fc = lax.all_gather(fc_weight, "fsdp", axis=0, tiled=True)
+    proj_flip = lax.all_gather(proj_weight.T, "fsdp", axis=0, tiled=True)
     columns = whole_qkv.shape[-1]
     heads_here = columns // HD
     total_rows = seq_count * seq_rows
@@ -167,43 +202,39 @@
             jnp.zeros((seq_count, seq_rows, heads_here), jnp.float32),
         ),
     )
-    mixed = attended.reshape(total_rows, columns).astype(jnp.bfloat16)
-    attn_out = (
-        lax.psum(jnp.dot(mixed, whole_out, preferred_element_type=jnp.float32), "tp") + out_bias
-    )
+    mixed_flip = attended.reshape(total_rows, columns).astype(jnp.bfloat16).T
+    all_mixed = lax.all_gather(mixed_flip, "tp", axis=0, tiled=True)
+    attn_out = jnp.einsum("ht,hd->td", all_mixed, all_out, preferred_element_type=jnp.float32) + out_bias
     middle = inputs + attn_out
     normed_two, scale_two = normalized(middle)
     act_two = (normed_two * ln2_gain + ln2_bias).astype(jnp.bfloat16)
     hidden_pre = jnp.dot(act_two, whole_fc, preferred_element_type=jnp.float32) + fc_bias
     hidden_out, gelu_back = jax.vjp(gelu_curve, hidden_pre)
     hidden = hidden_out.astype(jnp.bfloat16)
-    branch = (
-        lax.psum(
-            jnp.dot(hidden, whole_proj, preferred_element_type=jnp.float32).astype(jnp.bfloat16),
-            "tp",
-        ).astype(jnp.float32)
-        + proj_bias
-    )
-    result = (middle + branch).astype(jnp.bfloat16).reshape(seq_count, seq_rows, model_width)
+    branch_part = jnp.einsum(
+        "tf,df->td", hidden, proj_flip, preferred_element_type=jnp.float32
+    ).astype(jnp.bfloat16)
     upstream_low = out_grad.reshape(total_rows, model_width)
     upstream = upstream_low.astype(jnp.float32)
     proj_bias_grad = jnp.sum(upstream, axis=0)
-    proj_grad = jnp.einsum("tf,td->fd", hidden, upstream_low, preferred_element_type=jnp.float32)
-    hidden_grad = jnp.einsum(
-        "td,fd->tf", upstream_low, whole_proj, preferred_element_type=jnp.float32
-    )
+    proj_grad = jnp.einsum("td,tf->df", upstream_low, hidden, preferred_element_type=jnp.float32)
+    hidden_grad = jnp.dot(upstream_low, proj_flip, preferred_element_type=jnp.float32)
     pre_grad = gelu_back(hidden_grad)[0].astype(jnp.bfloat16)
     fc_bias_grad = jnp.sum(pre_grad.astype(jnp.float32), axis=0)
     fc_grad = jnp.einsum("td,tf->df", act_two, pre_grad, preferred_element_type=jnp.float32)
-    act_two_grad = lax.psum(
-        jnp.einsum("tf,df->td", pre_grad, whole_fc, preferred_element_type=jnp.float32), "tp"
-    )
-    ln2_gain_grad = jnp.sum(act_two_grad * normed_two, axis=0)
-    ln2_bias_grad = jnp.sum(act_two_grad, axis=0)
+    act_two_part = jnp.einsum("tf,df->td", pre_grad, whole_fc, preferred_element_type=jnp.float32)
+    ln2_gain_grad = jnp.sum(act_two_part * normed_two, axis=0)
+    ln2_bias_grad = jnp.sum(act_two_part, axis=0)
+    act_two_grad = lax.psum(act_two_part.astype(jnp.bfloat16), "tp").astype(jnp.float32)
+    act_two_grad, branch_part = lax.optimization_barrier((act_two_grad, branch_part))
+    branch_low = lax.psum(branch_part, "tp")
+    shard_fc = combine(scatter_rows(fc_grad[None], "fsdp"))[0]
+    shard_proj = combine(scatter_rows(proj_grad[None], "fsdp"))[0].T
     middle_grad = upstream + norm_back(act_two_grad, ln2_gain, normed_two, scale_two)
     attn_grad = middle_grad.astype(jnp.bfloat16)
     out_bias_grad = jnp.sum(attn_grad.astype(jnp.float32), axis=0)
-    out_grad_weight = jnp.einsum("th,td->hd", mixed, attn_grad, preferred_element_type=jnp.float32)
+    out_flip_grad = jnp.einsum("td,ht->dh", attn_grad, mixed_flip, preferred_element_type=jnp.float32)
+    shard_out = combine(scatter_rows(out_flip_grad[None], "fsdp"))[0].T
     mixed_grad = (
         jnp.einsum("td,hd->th", attn_grad, whole_out, preferred_element_type=jnp.float32)
         .astype(jnp.bfloat16)
@@ -219,12 +250,16 @@
             log_sums[sequence],
             visible,
         )
-        pair_grad = lax.psum_scatter(pair_term, "ctx", scatter_dimension=0, tiled=True)
         query_grads.append(query_grad)
-        pair_grads.append(pair_grad)
+        pair_grads.append(pair_term)
     query_grad_low = jnp.concatenate(query_grads, axis=0).astype(jnp.bfloat16)
-    pair_low = jnp.concatenate(pair_grads, axis=0).astype(jnp.bfloat16)
+    pair_low = (
+        scatter_rows(jnp.stack(pair_grads), "ctx")
+        .astype(jnp.bfloat16)
+        .reshape(total_rows, 2 * columns)
+    )
     stacked = jnp.stack([query_grad_low, pair_low[:, :columns], pair_low[:, columns:]])
+    branch_low, stacked = lax.optimization_barrier((branch_low, stacked))
     qv_bias_grad = jnp.stack(
         [
             jnp.sum(stacked[0].astype(jnp.float32), axis=0),
@@ -232,51 +267,45 @@
         ]
     )
     qkv_grad = jnp.einsum("td,cth->cdh", act_one, stacked, preferred_element_type=jnp.float32)
-    act_one_grad = lax.psum(
-        jnp.einsum("cth,cdh->td", stacked, whole_qkv, preferred_element_type=jnp.float32), "tp"
-    )
-    ln1_gain_grad = jnp.sum(act_one_grad * normed_one, axis=0)
-    ln1_bias_grad = jnp.sum(act_one_grad, axis=0)
+    act_one_part = jnp.einsum("cth,cdh->td", stacked, whole_qkv, preferred_element_type=jnp.float32)
+    ln1_gain_grad = jnp.sum(act_one_part * normed_one, axis=0)
+    ln1_bias_grad = jnp.sum(act_one_part, axis=0)
+    act_one_grad = lax.psum(act_one_part.astype(jnp.bfloat16), "tp").astype(jnp.float32)
+    shard_qkv = combine(scatter_rows(qkv_grad, "fsdp"))
+    norm_sums = sum_all(
+        jnp.concatenate([ln1_gain_grad, ln1_bias_grad, ln2_gain_grad, ln2_bias_grad]), "tp"
+    )
+    packed = jnp.concatenate(
+        [norm_sums, out_bias_grad, proj_bias_grad, fc_bias_grad, qv_bias_grad[0], qv_bias_grad[1]]
+    )
+    packed = sum_all(sum_all(packed, "fsdp"), "ctx")
+    hidden_here = fc_bias_grad.shape[0]
+    norm_sums = packed[: 6 * model_width].reshape(6, model_width)
+    fc_bias_sum = packed[6 * model_width : 6 * model_width + hidden_here]
+    qv_sum = packed[6 * model_width + hidden_here :].reshape(2, columns)
+    result = (
+        (middle + (branch_low.astype(jnp.float32) + proj_bias))
+        .astype(jnp.bfloat16)
+        .reshape(seq_count, seq_rows, model_width)
+    )
     tokens_grad = (middle_grad + norm_back(act_one_grad, ln1_gain, normed_one, scale_one)).reshape(
         seq_count, seq_rows, model_width
-    )
-    shard_qkv, shard_out, shard_fc, shard_proj = (
-        lax.psum_scatter(qkv_grad, "fsdp", scatter_dimension=1, tiled=True),
-        lax.psum_scatter(out_grad_weight, "fsdp", scatter_dimension=1, tiled=True),
-        lax.psum_scatter(fc_grad, "fsdp", scatter_dimension=0, tiled=True),
-        lax.psum_scatter(proj_grad, "fsdp", scatter_dimension=1, tiled=True),
-    )
-    shard_qkv, shard_out, shard_fc, shard_proj = lax.psum(
-        (shard_qkv, shard_out, shard_fc, shard_proj), "ctx"
-    )
-    small_sums = lax.psum(
-        (
-            ln1_gain_grad,
-            ln1_bias_grad,
-            qv_bias_grad,
-            out_bias_grad,
-            ln2_gain_grad,
-            ln2_bias_grad,
-            fc_bias_grad,
-            proj_bias_grad,
-        ),
-        ("fsdp", "ctx"),
     )
     return (
         result,
         tokens_grad,
-        small_sums[0],
-        small_sums[1],
+        norm_sums[0],
+        norm_sums[1],
         shard_qkv,
-        small_sums[2],
+        qv_sum,
         shard_out,
-        small_sums[3],
-        small_sums[4],
-        small_sums[5],
+        norm_sums[4],
+        norm_sums[2],
+        norm_sums[3],
         shard_fc,
-        small_sums[6],
+        fc_bias_sum,
         shard_proj,
-        small_sums[7],
+        norm_sums[5],
     )
 
 

time: 824 us -> 464 us (0.56)
  waiting for transfers between devices: 586 us -> 182 us
  local copies, waits for them, and re-layouts: 50.1 us -> 84.2 us
  blocking collectives: 46.3 us -> 20.9 us
  other arithmetic: 38.2 us -> 55.7 us
  starting transfers between devices: 1.22 us -> 18.6 us
    psum x5 -> x3, waiting for transfers between devices: 443 us -> 81.4 us  [the longest x1 46.2 us: body(): lax.psum(act_two_part.astype(jnp.bfloat16), 'tp').astype(jnp.float32)]
    reduce_scatter x4 -> x0, waiting for transfers between devices: 89.5 us -> none  [the longest x1 35.2 us: body(): lax.psum_scatter(fc_grad, 'fsdp', scatter_dimension=0, tiled=True)]
    all_gather x2 -> x4, waiting for transfers between devices: 0.01 us -> 56.7 us  [the longest x1 34.1 us: body(): all_mixed = lax.all_gather(mixed_flip, 'tp', axis=0, tiled=True)]
    unnamed x16 -> x8, waiting for transfers between devices: 32.1 us -> 1.15 us
    psum x1 -> x0, blocking collectives: 25.4 us -> none  [body(): lax.psum((ln1_gain_grad, ln1_bias_grad, qv_bias_grad, out_bias_grad, ln2_...]
    ppermute x0 -> x18, waiting for transfers between devices: none -> 23.5 us  [swap(): return lax.ppermute(values, axis_name, [(i, i ^ bit) for i in range(count)])]
    ppermute x0 -> x18, starting transfers between devices: none -> 18.1 us  [swap(): return lax.ppermute(values, axis_name, [(i, i ^ bit) for i in range(count)])]
    unnamed x126 -> x117, local copies, waits for them, and re-layouts: 33.5 us -> 19.3 us
  transfers between devices with their start and end apart: 14 -> 26, of which waited for: 10 -> 12; matrix products, arithmetic and copies ran while one was open for 12% -> 43% of each run, Pallas kernels for 0% -> 0%
where the time goes in v1:
time: 464 us; the launch traced here: 456 us
  waiting for transfers between devices  182 us (39%)
  local copies, waits for them, and re-layouts  84.2 us (18%)
  matrix products  78.5 us (17%)
  other arithmetic  55.7 us (12%)
  blocking collectives  20.9 us (5%)
  starting transfers between devices  18.6 us (4%)
  between operations  15.3 us (3%)
    psum x1, waiting for transfers between devices, body(): lax.psum(act_two_part.astype(jnp.bfloat16), 'tp').astype(jnp.float32)  46.2 us
    psum x1, waiting for transfers between devices, body(): lax.psum(act_one_part.astype(jnp.bfloat16), 'tp').astype(jnp.float32)  35.1 us
    all_gather x1, waiting for transfers between devices, body(): all_mixed = lax.all_gather(mixed_flip, 'tp', axis=0, tiled=True)  34.1 us
    ppermute x18, waiting for transfers between devices, swap(): return lax.ppermute(values, axis_name, [(i, i ^ bit) for i in range(count)])  23.5 us
    all_gather x1, waiting for transfers between devices, body(): pair_whole = lax.all_gather(key_value, 'ctx', axis=1, tiled=True)  19.8 us
    unnamed x117, local copies, waits for them, and re-layouts  19.3 us
    ppermute x18, starting transfers between devices, swap(): return lax.ppermute(values, axis_name, [(i, i ^ bit) for i in range(count)])  18.1 us
    all_gather x1, blocking collectives, body(): whole_qkv = lax.all_gather(qkv_weight, 'fsdp', axis=1, tiled=True)  14.3 us
  transfers between devices with their start and end apart: 26, of which 12 were waited for; matrix products, arithmetic and copies ran while one was open for 43% of the time, Pallas kernels for 0%

profile of v1, /device:TPU:0, one launch (start us, length us, event | category | flops | bytes accessed | tf_op | source)
XLA Modules:
  0.0 456.1 jit_solution(3788652275751168901)
XLA Ops:
  7.2 1.8 convert_reduce_fusion
  10.0 14.3 %all_gather.21 = bf16[3,768,192]{2,0,1:T(4,128)(2,1)S(1)} all-gather(bf16[3,192,192]{2,0,1:T(4,128)(2,1)S(1)} %copy.169), channel_id=1, replica_groups=mesh['fsdp'=4,'ctx'=2,'tp'=4] {'fsdp'}, dimensions={1}, use_global_device_ids=true | all-gather | bytes 1105920 | tf_op jit(solution)/shard_map/all_gather | solution.py:145
  24.4 2.1 copy.170
  32.7 6.6 %all_gather.24 = bf16[768,192]{1,0:T(8,128)(2,1)S(1)} all-gather(bf16[192,192]{1,0:T(8,128)(2,1)S(1)} %bitcast.251), channel_id=1, replica_groups=mesh['fsdp'=4,'ctx'=2,'tp'=4] {'fsdp'}, dimensions={0}, use_global_device_ids=true | all-gather | bytes 368640 | tf_op jit(solution)/shard_map/all_gather | solution.py:146
  40.9 19.8 %all-gather.6.cloned.1.call-done = bf16[2,1024,384]{1,2,0:T(8,128)(2,1)} async-done(((bf16[2,512,384]{1,2,0:T(8,128)(2,1)}), bf16[2,1024,384]{1,2,0:T(8,128)(2,1)}) %all-gather.6.cloned.1.call-update) | async-done | bytes 1572880 | tf_op jit(solution)/shard_map/all_gather | solution.py:161
  60.7 1.9 copy.174
  63.2 19.3 %while.54 = (s32[]{:T(128)}, bf16[2,512,192]{1,2,0:T(8,128)(2,1)S(1)}, f32[2,512,3]{1,2,0:T(4,128)}, bf16[2,512,192]{2,1,0:T(8,128)(2,1)S(1)}, bf16[2,1024,384]{...) while((s32[]{:T(128)}, ...), condition=%wide.region_6.7_spmd.clone, body=%wide.region_3.6_spmd.clone.sunk | while | flops 138935840 | bytes 7109057 | solution.py:196
  84.9 2.1 fusion.81
  88.9 2.1 copy.175
  93.7 2.0 reshape.449
  96.9 34.1 %all-gather.8.cloned.1.call-done = bf16[768,1024]{1,0:T(8,128)(2,1)} async-done(((bf16[192,1024]{1,0:T(8,128)(2,1)}), bf16[768,1024]{1,0:T(8,128)(2,1)}) %all-gather.8.cloned.1.call-update) | async-done | bytes 1572880 | tf_op jit(solution)/shard_map/all_gather | solution.py:206
  131.0 3.9 fusion.111
  135.6 1.7 add_convert_fusion.1
  137.3 11.5 %all-gather.14.cloned.1.call-done = bf16[768,768]{1,0:T(8,128)(2,1)} async-done(((bf16[192,768]{1,0:T(8,128)(2,1)}), bf16[768,768]{1,0:T(8,128)(2,1)}) %all-gather.14.cloned.1.call-update) | async-done | bytes 1179664 | tf_op jit(solution)/shard_map/all_gather | solution.py:148
  148.8 3.3 fusion.114
  152.1 1.9 fusion.102
  156.6 11.1 %all-gather.12.cloned.1.call-done = bf16[768,768]{1,0:T(8,128)(2,1)} async-done(((bf16[192,768]{1,0:T(8,128)(2,1)}), bf16[768,768]{1,0:T(8,128)(2,1)}) %all-gather.12.cloned.1.call-update) | async-done | bytes 1179664 | tf_op jit(solution)/shard_map/all_gather | solution.py:149
  167.7 6.4 %convert_reduce_fusion.1 = (f32[768]{0:T(1024)}, bf16[1024,768]{1,0:T(8,128)(2,1)S(1)}) fusion(f32[1024,768]{1,0:T(8,128)} %copy-done.57, f32[768]{0:T(1024)} %param.31, bf16[1024,768]{1,0:T(8,128)(2,1)} %bitcast.229, bf16[768,768]{1,0:T(8,128)(2,1)} %all-gather.12.cloned.1.call-done), kind=kOutput, calls=%fused_computation.97 | convolution fusion | flops 1226046720 | bytes 7477248 | tf_op jit(solution)/shard_map/dot_general | solution.py:221
  178.5 3.6 fusion.112
  182.2 1.7 bitcast_add_fusion.1
  189.0 4.9 %collective-permute-done.16 = bf16[1,1,192,768]{3,2,1,0:T(8,128)(2,1)S(1)} collective-permute-done((bf16[1,1,192,768]{3,2,1,0:T(8,128)(2,1)S(1)}, bf16[1,1,192,768]{3,2,1,0:T(8,128)(2,1)S(1)}, u32[]{:S(2)}, u32[]{:S(2)}) %collective-permute-start.16) | collective-permute-done | bytes 294944 | tf_op jit(solution)/shard_map/ppermute | solution.py:31
  196.1 3.3 convolution_convert_fusion
  199.6 1.9 fusion.88
  203.1 1.9 add_bitcast_fusion
  205.0 46.2 %all-reduce.4.cloned.1.call-done = bf16[1024,768]{1,0:T(8,128)(2,1)} async-done(((bf16[1024,768]{1,0:T(8,128)(2,1)}), bf16[1024,768]{1,0:T(8,128)(2,1)}) %all-reduce.4.cloned.1.call-update) | async-done | bytes 1572880 | tf_op jit(solution)/shard_map/psum | solution.py:228
  251.2 3.3 convert_element_type.385
  254.6 4.6 %multiply_reduce_fusion.2 = (f32[768]{0:T(1024)}, f32[1024]{0:T(1024)S(1)}, f32[1024]{0:T(1024)S(1)}, f32[768]{0:T(1024)}) fusion(f32[1024,768]{1,0:T(8,128)} %get-tuple-element.983, f32[1024,768]{1,0:T(8,128)S(1)} %get-tuple-element.981, f32[1024]{0:T(1024)S(1)} %add_rsqrt_fusion, f32[1024]{0:T(1024)S(1)} %broadcast_multiply_fusion.4, ...), kind=kLoop, calls=%fused_computation.100 | loop fusion | flops 7074304 | bytes 9462784 | tf_op jit(solution)/shard_map/reduce_sum | solution.py:226
  259.3 3.0 convert_bitcast_fusion.3
  262.2 2.6 copy.193
  264.8 2.7 convolution_convert_fusion.1
  270.3 23.0 %while.56 = (s32[]{:T(128)}, bf16[512,192]{0,1:T(8,128)(2,1)}, f32[1024,384]{0,1:T(8,128)}, bf16[512,192]{0,1:T(8,128)(2,1)S(1)}, bf16[1024,384]{1,0:T(8,128)(2,...) while((s32[]{:T(128)}, bf16[512,192]{0,1:T(8,128)(2,1)}, ...), condition=%wide.region_18.19_spmd.clone, body=%wide.region_16.18_spmd.clone.sunk | while | flops 340884992 | bytes 22167932 | solution.py:112
  271.1 1.5 fusion.189
  276.1 1.9 convolution_dynamic-update-slice_fusion.5
  278.8 1.5 fusion.189
  283.8 1.9 convolution_dynamic-update-slice_fusion.5
  286.4 1.5 fusion.189
  291.5 1.8 convolution_dynamic-update-slice_fusion.5
  293.3 3.1 copy.187
  298.5 20.5 %while.55 = (s32[]{:T(128)}, bf16[512,192]{0,1:T(8,128)(2,1)}, f32[1024,384]{0,1:T(8,128)}, bf16[512,192]{0,1:T(8,128)(2,1)S(1)}, bf16[1024,384]{1,0:T(8,128)(2,...) while((s32[]{:T(128)}, bf16[512,192]{0,1:T(8,128)(2,1)}, ...), condition=%wide.region_15.16_spmd.clone, body=%wide.region_13.15_spmd.clone.sunk | while | flops 340884992 | bytes 22167932 | solution.py:112
  319.1 3.0 copy.186
  322.1 1.6 fusion.80
  326.0 2.1 add_bitcast_fusion.1
  330.4 11.9 %collective-permute-done = bf16[2,1,512,384]{3,2,0,1:T(8,128)(2,1)S(1)} collective-permute-done((bf16[2,1,512,384]{3,2,0,1:T(8,128)(2,1)S(1)}, bf16[2,1,512,384]{3,2,0,1:T(8,128)(2,1)S(1)}, u32[]{:S(2)}, u32[]{:S(2)}) %collective-permute-start) | collective-permute-done | bytes 786464 | tf_op jit(solution)/shard_map/ppermute | solution.py:31
  344.9 2.0 copy.206
  346.9 2.3 pad_maximum_fusion
  349.1 5.2 %bitcast_convert_fusion = (bf16[1024,768]{1,0:T(8,128)(2,1)}, f32[1024,768,1]{1,0,2:T(8,128)}) fusion(bf16[3,1024,192]{1,2,0:T(8,128)(2,1)} %pad_maximum_fusion, bf16[3,768,192]{1,2,0:T(8,128)(2,1)} %copy.170), kind=kOutput, calls=%fused_computation.79 | convolution fusion | flops 906756096 | bytes 6782976 | tf_op jit(solution)/shard_map/cth,cdh->td/dot_general | solution.py:270
  354.4 1.6 fusion.91
  357.4 4.1 fusion.77
  361.5 4.7 %reshape_reshape.4 = f32[3,2,2,192,192]{3,2,1,4,0:T(2,128)} reshape(f32[3,768,192]{1,2,0:T(8,128)} %fusion.77) | data formatting | bytes 3538944 | tf_op jit(solution)/shard_map/reshape;reshape | solution.py:50
  366.2 3.8 constant_dynamic-slice_fusion.2
  370.0 3.6 copy.207
  375.3 3.8 constant_dynamic-slice_fusion.3
  379.1 3.7 copy.191
  384.2 1.6 bitcast_add_fusion.3
  386.8 1.6 collective-permute-start.7
  388.4 35.1 %all-reduce.8.cloned.1.call-done = bf16[1024,768]{1,0:T(8,128)(2,1)} async-done(((bf16[1024,768]{1,0:T(8,128)(2,1)}), bf16[1024,768]{1,0:T(8,128)(2,1)}) %all-reduce.8.cloned.1.call-update) | async-done | bytes 1572880 | tf_op jit(solution)/shard_map/psum | solution.py:273
  423.6 3.7 fusion.55
  428.3 2.8 collective-permute-done.1
  431.2 1.6 collective-permute-start.2
  432.8 2.5 convert_reduce_fusion.3
  437.2 1.5 collective-permute-start.8
  438.7 1.5 collective-permute-start.4
  440.3 2.9 add_convert_fusion
  443.8 3.1 collective-permute-done.8
  (328 shorter events, 109.4 us)
Async XLA Ops:
  7.2 53.5 %all-gather.6.cloned.1.call-start = ((), (), s32[]{:S(2)}) async-start(), calls=%async_computation | async-start | bytes 2359296 | tf_op jit(solution)/shard_map/all_gather | solution.py:161
  9.1 17.4 %copy-start.35 = (f32[1,4,2,128]{3,1,2,0:T(4,128)}, f32[1,4,2,128]{3,1,2,0:T(4,128)S(1)}, u32[]{:S(2)}) copy-start(f32[1,4,2,128]{3,1,2,0:T(4,128)S(1)} %copy.228) | copy-start | bytes 12292
  9.7 16.7 %copy-start.37 = (f32[1,4,2,128]{3,1,2,0:T(4,128)}, f32[1,4,2,128]{3,1,2,0:T(4,128)S(1)}, u32[]{:S(2)}) copy-start(f32[1,4,2,128]{3,1,2,0:T(4,128)S(1)} %copy.229) | copy-start | bytes 12292
  10.0 16.4 %copy-start.43 = (f32[768]{0:T(1024)S(1)}, f32[768]{0:T(1024)}, u32[]{:S(2)}) copy-start(f32[768]{0:T(1024)} %param.22) | copy-start | bytes 9220
  10.0 16.4 %copy-start.46 = (f32[768]{0:T(1024)S(1)}, f32[768]{0:T(1024)}, u32[]{:S(2)}) copy-start(f32[768]{0:T(1024)} %param.23) | copy-start | bytes 9220
  31.6 8.7 %copy-start.51 = (s32[4]{0:T(128)S(1)}, s32[4]{0:T(128)}, u32[]{:S(2)}) copy-start(s32[4]{0:T(128)} %param.34) | copy-start | bytes 52
  32.5 64.4 %all-gather.10.cloned.1.call-start = ((), (), s32[]{:S(2)}) async-start(), calls=%async_computation.2 | async-start | bytes 1474560 | tf_op jit(solution)/shard_map/all_gather | solution.py:147
  40.2 90.9 %all-gather.8.cloned.1.call-start = ((), (), s32[]{:S(2)}) async-start(), calls=%async_computation.1 | async-start | bytes 1966080 | tf_op jit(solution)/shard_map/all_gather | solution.py:206
  82.6 4.4 copy-start.10
  83.4 65.4 %all-gather.14.cloned.1.call-start = ((), (), s32[]{:S(2)}) async-start(), calls=%async_computation.4 | async-start | bytes 1474560 | tf_op jit(solution)/shard_map/all_gather | solution.py:148
  84.0 83.7 %all-gather.12.cloned.1.call-start = ((), (), s32[]{:S(2)}) async-start(), calls=%async_computation.3 | async-start | bytes 1474560 | tf_op jit(solution)/shard_map/all_gather | solution.py:149
  84.6 166.7 %all-reduce.4.cloned.1.call-start = ((), (), s32[]{:S(2)}) async-start(), calls=%async_computation.5 | async-start | bytes 3145728 | tf_op jit(solution)/shard_map/psum | solution.py:228
  84.9 6.2 %copy-start.8 = (bf16[2,1024,384]{1,2,0:T(8,128)(2,1)S(1)}, bf16[2,1024,384]{1,2,0:T(8,128)(2,1)}, u32[]{:S(2)}) copy-start(bf16[2,1024,384]{1,2,0:T(8,128)(2,1)} %all-gather.6.cloned.1.call-done) | copy-start | bytes 4718596
  91.2 39.8 %copy-start.54 = (f32[768]{0:T(1024)S(1)}, f32[768]{0:T(1024)}, u32[]{:S(2)}) copy-start(f32[768]{0:T(1024)} %param.27) | copy-start | bytes 9220
  148.8 3.3 copy-start.11
  148.8 3.3 copy-start.55
  156.4 25.8 %collective-permute-start.15 = (bf16[1,2,192,768]{3,2,1,0:T(8,128)(2,1)}, bf16[1,2,192,768]{3,2,1,0:T(8,128)(2,1)}, u32[]{:S(2)}, u32[]{:S(2)}) collective-permute-start(bf16[1,2,192,768]{3,2,1,0:T(8,128)(2,1)} %fusion.84), channel_id=1, source_target_pairs={{0,8},{8,0},{16,24},{24,16},{1,9},{9,1},{17,25},{25,17},{2,10},{10... | collective-permute-start | bytes 1769480 | tf_op jit(solution)/shard_map/ppermute | solution.py:31
  167.7 6.4 %copy-start.21 = (bf16[1024,768]{1,0:T(8,128)(2,1)S(1)}, bf16[1024,768]{1,0:T(8,128)(2,1)}, u32[]{:S(2)}) copy-start(bf16[1024,768]{1,0:T(8,128)(2,1)} %add_convert_fusion.1) | copy-start | bytes 4718596
  174.1 4.4 copy-start.53
  177.8 6.5 %collective-permute-start.12 = (bf16[1,2,192,768]{3,2,1,0:T(8,128)(2,1)}, bf16[1,2,192,768]{3,2,1,0:T(8,128)(2,1)}, u32[]{:S(2)}, u32[]{:S(2)}) collective-permute-start(bf16[1,2,192,768]{3,2,1,0:T(8,128)(2,1)} %fusion.83), channel_id=1, source_target_pairs={{0,8},{8,0},{16,24},{24,16},{1,9},{9,1},{17,25},{25,17},{2,10},{10... | collective-permute-start | bytes 1769480 | tf_op jit(solution)/shard_map/ppermute | solution.py:31
  182.1 167.1 %all-reduce.6.cloned.1.call-start = ((), (), s32[]{:S(2)}) async-start(), calls=%async_computation.6 | async-start | bytes 3145728 | tf_op jit(solution)/shard_map/psum | solution.py:230
  183.9 12.2 %copy-start.52 = (bf16[768,768]{1,0:T(8,128)(2,1)S(1)}, bf16[768,768]{1,0:T(8,128)(2,1)}, u32[]{:S(2)}) copy-start(bf16[768,768]{1,0:T(8,128)(2,1)} %all-gather.12.cloned.1.call-done) | copy-start | bytes 3538948
  183.9 12.2 %copy-start.56 = (f32[768]{0:T(1024)S(1)}, f32[768]{0:T(1024)}, u32[]{:S(2)}) copy-start(f32[768]{0:T(1024)} %param.31) | copy-start | bytes 9220
  183.9 12.2 %copy-start.58 = (f32[1024,768]{1,0:T(8,128)S(1)}, f32[1024,768]{1,0:T(8,128)}, u32[]{:S(2)}) copy-start(f32[1024,768]{1,0:T(8,128)} %copy-done.57) | copy-start | bytes 9437188
  184.0 9.9 %collective-permute-start.16 = (bf16[1,1,192,768]{3,2,1,0:T(8,128)(2,1)S(1)}, bf16[1,1,192,768]{3,2,1,0:T(8,128)(2,1)S(1)}, u32[]{:S(2)}, u32[]{:S(2)}) collective-permute-start(bf16[1,1,192,768]{3,2,1,0:T(8,128)(2,1)S(1)} %dynamic-slice_convert_fusion), channel_id=1, source_target_pairs={{0,16},{8,24},{16,0},{24,8},{1,17},{9,25},{17,1},{25,9},{2,18},{10... | collective-permute-start | bytes 884744 | tf_op jit(solution)/shard_map/ppermute | solution.py:31
  187.5 12.1 %collective-permute-start.13 = (bf16[1,1,192,768]{3,2,1,0:T(8,128)(2,1)}, bf16[1,1,192,768]{3,2,1,0:T(8,128)(2,1)}, u32[]{:S(2)}, u32[]{:S(2)}) collective-permute-start(bf16[1,1,192,768]{3,2,1,0:T(8,128)(2,1)} %dynamic-slice_convert_fusion.1), channel_id=1, source_target_pairs={{0,16},{8,24},{16,0},{24,8},{1,17},{9,25},{17,1},{25,9},{2,18},{10... | collective-permute-start | bytes 884744 | tf_op jit(solution)/shard_map/ppermute | solution.py:31
  194.7 8.4 %collective-permute-start.17 = (bf16[1,192,768]{2,1,0:T(8,128)(2,1)}, bf16[1,192,768]{2,1,0:T(8,128)(2,1)}, u32[]{:S(2)}, u32[]{:S(2)}) collective-permute-start(bf16[1,192,768]{2,1,0:T(8,128)(2,1)} %fusion.89), channel_id=1, source_target_pairs={{0,4},{4,0},{1,5},{5,1},{2,6},{6,2},{3,7},{7,3},{8,12},{12,8},{9,1... | collective-permute-start | bytes 884744 | tf_op jit(solution)/shard_map/ppermute | solution.py:31
  201.6 124.4 %collective-permute-start.14 = (bf16[1,192,768]{2,1,0:T(8,128)(2,1)}, bf16[1,192,768]{2,1,0:T(8,128)(2,1)}, u32[]{:S(2)}, u32[]{:S(2)}) collective-permute-start(bf16[1,192,768]{2,1,0:T(8,128)(2,1)} %fusion.88), channel_id=1, source_target_pairs={{0,4},{4,0},{1,5},{5,1},{2,6},{6,2},{3,7},{7,3},{8,12},{12,8},{9,1... | collective-permute-start | bytes 884744 | tf_op jit(solution)/shard_map/ppermute | solution.py:31
  254.5 169.0 %all-reduce.8.cloned.1.call-start = ((), (), s32[]{:S(2)}) async-start(), calls=%async_computation.7 | async-start | bytes 3145728 | tf_op jit(solution)/shard_map/psum | solution.py:273
  254.6 4.7 %copy-start.4 = (f32[1024,768]{1,0:T(8,128)S(1)}, f32[1024,768]{1,0:T(8,128)}, u32[]{:S(2)}) copy-start(f32[1024,768]{1,0:T(8,128)} %convert_element_type.385) | copy-start | bytes 9437188
  254.6 4.7 %copy-start.12 = (bf16[2,512,768]{2,1,0:T(8,128)(2,1)S(1)}, bf16[2,512,768]{2,1,0:T(8,128)(2,1)}, u32[]{:S(2)}) copy-start(bf16[2,512,768]{2,1,0:T(8,128)(2,1)} %param.35) | copy-start | bytes 4718596
  254.6 4.6 %copy-start.40 = (f32[768]{0:T(1024)S(1)}, f32[768]{0:T(1024)}, u32[]{:S(2)}) copy-start(f32[768]{0:T(1024)} %param.28) | copy-start | bytes 9220
  275.1 2.9 copy-start.32
  282.8 2.9 copy-start.32
  290.5 2.9 copy-start.32
  293.3 5.2 %copy-start.14 = (bf16[512,192]{0,1:T(8,128)(2,1)S(1)}, bf16[512,192]{0,1:T(8,128)(2,1)}, u32[]{:S(2)}) copy-start(bf16[512,192]{0,1:T(8,128)(2,1)} %get-tuple-element.1207) | copy-start | bytes 589828
  322.1 3.2 copy-start.9
  322.1 3.2 copy-start.22
  323.8 18.5 %collective-permute-start = (bf16[2,1,512,384]{3,2,0,1:T(8,128)(2,1)S(1)}, bf16[2,1,512,384]{3,2,0,1:T(8,128)(2,1)S(1)}, u32[]{:S(2)}, u32[]{:S(2)}) collective-permute-start(bf16[2,1,512,384]{3,2,0,1:T(8,128)(2,1)S(1)} %fusion.80), channel_id=1, source_target_pairs={{0,4},{4,0},{1,5},{5,1},{2,6},{6,2},{3,7},{7,3},{8,12},{12,8},{9,1... | collective-permute-start | bytes 2359304 | tf_op jit(solution)/shard_map/ppermute | solution.py:31
  325.3 17.0 %copy-start.6 = (f32[1024,384]{1,0:T(8,128)S(1)}, f32[1024,384]{1,0:T(8,128)}, u32[]{:S(2)}) copy-start(f32[1024,384]{1,0:T(8,128)} %copy.187) | copy-start | bytes 4718596
  325.3 17.0 %copy-start.7 = (f32[1024,384]{1,0:T(8,128)S(1)}, f32[1024,384]{1,0:T(8,128)}, u32[]{:S(2)}) copy-start(f32[1024,384]{1,0:T(8,128)} %copy.186) | copy-start | bytes 4718596
  325.9 2.2 collective-permute-start.9
  328.9 25.5 %collective-permute-start.10 = (bf16[1,1,192,192]{3,2,1,0:T(8,128)(2,1)}, bf16[1,1,192,192]{3,2,1,0:T(8,128)(2,1)}, u32[]{:S(2)}, u32[]{:S(2)}) collective-permute-start(bf16[1,1,192,192]{3,2,1,0:T(8,128)(2,1)} %dynamic-slice_convert_fusion.4), channel_id=1, source_target_pairs={{0,16},{8,24},{16,0},{24,8},{1,17},{9,25},{17,1},{25,9},{2,18},{10... | collective-permute-start | bytes 221192 | tf_op jit(solution)/shard_map/ppermute | solution.py:31
  349.1 5.2 %copy-start.27 = (f32[1,2,192,192]{3,2,1,0:T(8,128)S(1)}, f32[1,2,192,192]{3,2,1,0:T(8,128)}, u32[]{:S(2)}) copy-start(f32[1,2,192,192]{3,2,1,0:T(8,128)} %copy-done.26) | copy-start | bytes 884740
  355.9 17.7 %collective-permute-start.11 = (bf16[1,192,192]{2,1,0:T(8,128)(2,1)}, bf16[1,192,192]{2,1,0:T(8,128)(2,1)S(1)}, u32[]{:S(2)}, u32[]{:S(2)}) collective-permute-start(bf16[1,192,192]{2,1,0:T(8,128)(2,1)} %fusion.91), channel_id=1, source_target_pairs={{0,4},{4,0},{1,5},{5,1},{2,6},{6,2},{3,7},{7,3},{8,12},{12,8},{9,1... | collective-permute-start | bytes 221192 | tf_op jit(solution)/shard_map/ppermute | solution.py:31
  373.6 10.6 %collective-permute-start.6 = (bf16[3,2,192,192]{3,2,0,1:T(8,128)(2,1)}, bf16[3,2,192,192]{3,2,0,1:T(8,128)(2,1)}, u32[]{:S(2)}, u32[]{:S(2)}) collective-permute-start(bf16[3,2,192,192]{3,2,0,1:T(8,128)(2,1)} %bitcast.250), channel_id=1, source_target_pairs={{0,8},{8,0},{16,24},{24,16},{1,9},{9,1},{17,25},{25,17},{2,10},{10... | collective-permute-start | bytes 1327112 | tf_op jit(solution)/shard_map/ppermute | solution.py:31
  382.8 40.7 %copy-start.36 = (f32[1,4,2,128]{3,1,2,0:T(4,128)S(1)}, f32[1,4,2,128]{3,1,2,0:T(4,128)}, u32[]{:S(2)}) copy-start(f32[1,4,2,128]{3,1,2,0:T(4,128)} %copy-done.35) | copy-start | bytes 12292
  382.8 40.7 %copy-start.38 = (f32[1,4,2,128]{3,1,2,0:T(4,128)S(1)}, f32[1,4,2,128]{3,1,2,0:T(4,128)}, u32[]{:S(2)}) copy-start(f32[1,4,2,128]{3,1,2,0:T(4,128)} %copy-done.37) | copy-start | bytes 12292
  382.8 40.7 %copy-start.44 = (f32[768]{0:T(1024)S(1)}, f32[768]{0:T(1024)}, u32[]{:S(2)}) copy-start(f32[768]{0:T(1024)} %param.22) | copy-start | bytes 9220
  386.8 49.1 %collective-permute-start.7 = (bf16[3,1,192,192]{3,2,0,1:T(8,128)(2,1)S(1)}, bf16[3,1,192,192]{3,2,0,1:T(8,128)(2,1)}, u32[]{:S(2)}, u32[]{:S(2)}) collective-permute-start(bf16[3,1,192,192]{3,2,0,1:T(8,128)(2,1)S(1)} %dynamic-slice_convert_fusion.2), channel_id=1, source_target_pairs={{0,16},{8,24},{16,0},{24,8},{1,17},{9,25},{17,1},{25,9},{2,18},{10... | collective-permute-start | bytes 663560 | tf_op jit(solution)/shard_map/ppermute | solution.py:31
  423.5 3.8 copy-start.41
  423.5 3.8 copy-start.42
  423.5 9.3 %copy-start.1 = (bf16[2,512,768]{2,1,0:T(8,128)(2,1)S(1)}, bf16[2,512,768]{2,1,0:T(8,128)(2,1)}, u32[]{:S(2)}) copy-start(bf16[2,512,768]{2,1,0:T(8,128)(2,1)} %param.21) | copy-start | bytes 4718596
  423.5 9.3 %copy-start.5 = (f32[1024,768]{1,0:T(8,128)S(1)}, f32[1024,768]{1,0:T(8,128)}, u32[]{:S(2)}) copy-start(f32[1024,768]{1,0:T(8,128)} %get-tuple-element.946) | copy-start | bytes 9437188
  423.6 9.3 %copy-start.13 = (bf16[1024,768]{1,0:T(8,128)(2,1)S(1)}, bf16[1024,768]{1,0:T(8,128)(2,1)}, u32[]{:S(2)}) copy-start(bf16[1024,768]{1,0:T(8,128)(2,1)} %all-reduce.8.cloned.1.call-done) | copy-start | bytes 4718596
  427.4 3.8 collective-permute-start.1
  431.1 4.7 %copy-start.45 = (f32[768]{0:T(1024)S(1)}, f32[768]{0:T(1024)}, u32[]{:S(2)}) copy-start(f32[768]{0:T(1024)} %convert_reduce_fusion.2) | copy-start | bytes 9220
  431.1 4.7 %copy-start.48 = (f32[768]{0:T(1024)S(1)}, f32[768]{0:T(1024)}, u32[]{:S(2)}) copy-start(f32[768]{0:T(1024)} %get-tuple-element.947) | copy-start | bytes 9220
  431.2 9.1 %copy-start.49 = (f32[768]{0:T(1024)S(1)}, f32[768]{0:T(1024)}, u32[]{:S(2)}) copy-start(f32[768]{0:T(1024)} %param.33) | copy-start | bytes 9220
  431.2 4.7 %collective-permute-start.2 = (f32[3072]{0:T(1024)S(1)}, f32[3072]{0:T(1024)S(1)}, u32[]{:S(2)}, u32[]{:S(2)}) collective-permute-start(f32[3072]{0:T(1024)S(1)} %fusion.139), channel_id=1, source_target_pairs={{0,2},{1,3},{2,0},{3,1},{4,6},{5,7},{6,4},{7,5},{8,10},{9,11},{10,... | collective-permute-start | bytes 36872 | tf_op jit(solution)/shard_map/ppermute | solution.py:31
  435.9 2.8 collective-permute-start.3
  437.2 9.7 %collective-permute-start.8 = (bf16[3,192,192]{2,1,0:T(8,128)(2,1)S(1)}, bf16[3,192,192]{2,1,0:T(8,128)(2,1)S(1)}, u32[]{:S(2)}, u32[]{:S(2)}) collective-permute-start(bf16[3,192,192]{2,1,0:T(8,128)(2,1)S(1)} %fusion.87), channel_id=1, source_target_pairs={{0,4},{4,0},{1,5},{5,1},{2,6},{6,2},{3,7},{7,3},{8,12},{12,8},{9,1... | collective-permute-start | bytes 663560 | tf_op jit(solution)/shard_map/ppermute | solution.py:31
  438.7 4.5 collective-permute-start.4
  443.2 4.6 %collective-permute-start.5 = (f32[5760]{0:T(1024)S(1)}, f32[5760]{0:T(1024)S(1)}, u32[]{:S(2)}, u32[]{:S(2)}) collective-permute-start(f32[5760]{0:T(1024)S(1)} %add.544), channel_id=1, source_target_pairs={{0,4},{4,0},{1,5},{5,1},{2,6},{6,2},{3,7},{7,3},{8,12},{12,8},{9,1... | collective-permute-start | bytes 69128 | tf_op jit(solution)/shard_map/ppermute | solution.py:31
  (33 other events, 52.9 us)
Sparse Core Ops, SparseCore 0:
  32.6 28.0 all-gather.5
  62.3 30.2 all-gather.9
  94.8 36.2 all-gather.7
  132.5 16.2 all-gather.13
  150.2 17.4 all-gather.11
  182.2 68.9 all-reduce.3
  254.7 68.1 all-reduce.5
  354.5 68.9 all-reduce.7

commit v2 on v1

--- a/solution.py
+++ b/solution.py
@@ -1,6 +1,8 @@
 import jax
 import jax.numpy as jnp
 from jax import lax
+from jax.experimental import pallas as pl
+from jax.experimental.pallas import tpu as pltpu
 from jax.sharding import PartitionSpec as P
 
 HD = 64
@@ -60,6 +62,123 @@
     if lax.axis_size("ctx") == 2:
         return low.astype(jnp.float32) + swap(low, "ctx", 1).astype(jnp.float32)
     return lax.psum(low, "ctx").astype(jnp.float32)
+
+
+NT = (((1,), (1,)), ((), ()))
+NN = (((1,), (0,)), ((), ()))
+
+
+def dot(left, right, dims=NN):
+    return lax.dot_general(left, right, dims, preferred_element_type=jnp.float32)
+
+
+def flip(values):
+    return values.astype(jnp.float32).T.astype(jnp.bfloat16)
+
+
+def attend_kernel(query_ref, pair_ref, here_ref, all_ref, out_ref, lse_ref):
+    columns = query_ref.shape[2]
+    visible = here_ref[...] >= all_ref[...]
+    for head in range(columns // HD):
+        start = head * HD
+        query = query_ref[0, :, start : start + HD]
+        key = pair_ref[0, :, start : start + HD]
+        value = pair_ref[0, :, columns + start : columns + start + HD]
+        scores = jnp.where(visible, dot(key, query, NT) * 0.125, -1e30)
+        top = jnp.max(scores, axis=0, keepdims=True)
+        weights = jnp.exp(scores - top)
+        total = jnp.sum(weights, axis=0, keepdims=True)
+        prob_low = (weights * (1.0 / total)).astype(jnp.bfloat16)
+        out_ref[start : start + HD, :] = dot(flip(value), prob_low).astype(jnp.bfloat16)
+        lse_ref[0, head : head + 1, :] = top + jnp.log(total)
+
+
+def attend(query, pair, place_here, place_all):
+    count, rows, columns = query.shape
+    length = pair.shape[1]
+    heads = columns // HD
+    return pl.pallas_call(
+        attend_kernel,
+        grid=(count,),
+        in_specs=[
+            pl.BlockSpec((1, rows, columns), lambda s: (s, 0, 0)),
+            pl.BlockSpec((1, length, 2 * columns), lambda s: (s, 0, 0)),
+            pl.BlockSpec((1, rows), lambda s: (0, 0)),
+            pl.BlockSpec((length, 1), lambda s: (0, 0)),
+        ],
+        out_specs=[
+            pl.BlockSpec((columns, rows), lambda s: (0, s)),
+            pl.BlockSpec((1, heads, rows), lambda s: (s, 0, 0)),
+        ],
+        out_shape=[
+            jax.ShapeDtypeStruct((columns, count * rows), jnp.bfloat16),
+            jax.ShapeDtypeStruct((count, heads, rows), jnp.float32),
+        ],
+        compiler_params=pltpu.CompilerParams(vmem_limit_bytes=40 * 1024 * 1024),
+        cost_estimate=pl.CostEstimate(
+            flops=20 * count * rows * length * columns,
+            bytes_accessed=count * (rows + 2 * length) * columns * 2,
+            transcendentals=count * rows * length * heads,
+        ),
+        name="attend",
+    )(query, pair, place_here[None, :], place_all[:, None])
+
+
+def attend_back_kernel(
+    query_ref, pair_ref, grad_ref, lse_ref, here_ref, all_ref, query_grad_ref, term_ref
+):
+    columns = query_ref.shape[2]
+    visible = here_ref[...] >= all_ref[...]
+    query_parts, key_parts, value_parts = [], [], []
+    for head in range(columns // HD):
+        start = head * HD
+        query = query_ref[0, :, start : start + HD]
+        key = pair_ref[0, :, start : start + HD]
+        value = pair_ref[0, :, columns + start : columns + start + HD]
+        grad = grad_ref[0, :, start : start + HD]
+        scores = jnp.where(visible, dot(key, query, NT) * 0.125, -1e30)
+        prob = jnp.exp(scores - lse_ref[0, head : head + 1, :])
+        value_parts.append(dot(prob.astype(jnp.bfloat16), grad))
+        weighted = dot(value, grad, NT)
+        delta = jnp.sum(prob * weighted, axis=0, keepdims=True)
+        score_grad = (prob * (weighted - delta)).astype(jnp.bfloat16)
+        key_parts.append(dot(score_grad, query) * 0.125)
+        query_parts.append(dot(flip(key), score_grad) * 0.125)
+    query_grad_ref[0] = jnp.concatenate(query_parts, axis=0).T.astype(jnp.bfloat16)
+    term_ref[0] = jnp.concatenate(key_parts + value_parts, axis=1)
+
+
+def attend_back(query, pair, grad, lse, place_here, place_all):
+    count, rows, columns = query.shape
+    length = pair.shape[1]
+    heads = columns // HD
+    return pl.pallas_call(
+        attend_back_kernel,
+        grid=(count,),
+        in_specs=[
+            pl.BlockSpec((1, rows, columns), lambda s: (s, 0, 0)),
+            pl.BlockSpec((1, length, 2 * columns), lambda s: (s, 0, 0)),
+            pl.BlockSpec((1, rows, columns), lambda s: (s, 0, 0)),
+            pl.BlockSpec((1, heads, rows), lambda s: (s, 0, 0)),
+            pl.BlockSpec((1, rows), lambda s: (0, 0)),
+            pl.BlockSpec((length, 1), lambda s: (0, 0)),
+        ],
+        out_specs=[
+            pl.BlockSpec((1, rows, columns), lambda s: (s, 0, 0)),
+            pl.BlockSpec((1, length, 2 * columns), lambda s: (s, 0, 0)),
+        ],
+        out_shape=[
+            jax.ShapeDtypeStruct((count, rows, columns), jnp.bfloat16),
+            jax.ShapeDtypeStruct((count, length, 2 * columns), jnp.float32),
+        ],
+        compiler_params=pltpu.CompilerParams(vmem_limit_bytes=48 * 1024 * 1024),
+        cost_estimate=pl.CostEstimate(
+            flops=50 * count * rows * length * columns,
+            bytes_accessed=count * (2 * rows + 4 * length) * columns * 2,
+            transcendentals=count * rows * length * heads,
+        ),
+        name="attend_back",
+    )(query, pair, grad, lse, place_here[None, :], place_all[:, None])
 
 
 def query_side(query_rows, pair_rows, grad_rows, lse_rows, visible):
@@ -143,10 +262,10 @@
     place_here = lax.dynamic_slice_in_dim(place_all, lax.axis_index("ctx") * seq_rows, seq_rows)
     visible = place_here[:, None] >= place_all[None, :]
     whole_qkv = lax.all_gather(qkv_weight, "fsdp", axis=1, tiled=True)
-    whole_out = lax.all_gather(out_weight.T, "fsdp", axis=0, tiled=True).T
-    all_out = lax.all_gather(whole_out, "tp", axis=0, tiled=True)
-    whole_fc = lax.all_gather(fc_weight, "fsdp", axis=0, tiled=True)
-    proj_flip = lax.all_gather(proj_weight.T, "fsdp", axis=0, tiled=True)
+    hidden_cols = fc_weight.shape[1]
+    packed_weights = lax.all_gather(
+        jnp.concatenate([fc_weight, proj_weight.T, out_weight.T], axis=1), "fsdp", axis=0, tiled=True
+    )
     columns = whole_qkv.shape[-1]
     heads_here = columns // HD
     total_rows = seq_count * seq_rows
@@ -159,6 +278,11 @@
     value = (proj_qkv[2] + qv_bias[1]).astype(jnp.bfloat16)
     key_value = jnp.concatenate([key, value], axis=1).reshape(seq_count, seq_rows, 2 * columns)
     pair_whole = lax.all_gather(key_value, "ctx", axis=1, tiled=True)
+    packed_weights, query = lax.optimization_barrier((packed_weights, query))
+    whole_fc = packed_weights[:, :hidden_cols]
+    proj_flip = packed_weights[:, hidden_cols : 2 * hidden_cols]
+    whole_out = packed_weights[:, 2 * hidden_cols :].T
+    all_out = lax.all_gather(whole_out, "tp", axis=0, tiled=True)
     query_three = query.reshape(seq_count, seq_rows, columns)
     anchor = jnp.zeros((), jnp.int32)
 
@@ -193,16 +317,20 @@
         )
         return (attended, log_sums)
 
-    attended, log_sums = lax.fori_loop(
-        0,
-        seq_count * heads_here,
-        forward_item,
-        (
-            jnp.zeros((seq_count, seq_rows, columns), jnp.float32),
-            jnp.zeros((seq_count, seq_rows, heads_here), jnp.float32),
-        ),
-    )
-    mixed_flip = attended.reshape(total_rows, columns).astype(jnp.bfloat16).T
+    in_kernel = length * seq_rows <= 1024 * 1024
+    if in_kernel:
+        mixed_flip, log_sums = attend(query_three, pair_whole, place_here, place_all)
+    else:
+        attended, log_sums = lax.fori_loop(
+            0,
+            seq_count * heads_here,
+            forward_item,
+            (
+                jnp.zeros((seq_count, seq_rows, columns), jnp.float32),
+                jnp.zeros((seq_count, seq_rows, heads_here), jnp.float32),
+            ),
+        )
+        mixed_flip = attended.reshape(total_rows, columns).astype(jnp.bfloat16).T
     all_mixed = lax.all_gather(mixed_flip, "tp", axis=0, tiled=True)
     attn_out = jnp.einsum("ht,hd->td", all_mixed, all_out, preferred_element_type=jnp.float32) + out_bias
     middle = inputs + attn_out
@@ -240,23 +368,28 @@
         .astype(jnp.bfloat16)
         .reshape(seq_count, seq_rows, columns)
     )
-    query_grads = []
-    pair_grads = []
-    for sequence in range(seq_count):
-        query_grad, pair_term, delta_cols = query_side(
-            query_three[sequence],
-            pair_whole[sequence],
-            mixed_grad[sequence],
-            log_sums[sequence],
-            visible,
-        )
-        query_grads.append(query_grad)
-        pair_grads.append(pair_term)
-    query_grad_low = jnp.concatenate(query_grads, axis=0).astype(jnp.bfloat16)
+    if in_kernel:
+        query_grad_low, pair_terms = attend_back(
+            query_three, pair_whole, mixed_grad, log_sums, place_here, place_all
+        )
+        query_grad_low = query_grad_low.reshape(total_rows, columns)
+    else:
+        query_grads = []
+        pair_grads = []
+        for sequence in range(seq_count):
+            query_grad, pair_term, delta_cols = query_side(
+                query_three[sequence],
+                pair_whole[sequence],
+                mixed_grad[sequence],
+                log_sums[sequence],
+                visible,
+            )
+            query_grads.append(query_grad)
+            pair_grads.append(pair_term)
+        query_grad_low = jnp.concatenate(query_grads, axis=0).astype(jnp.bfloat16)
+        pair_terms = jnp.stack(pair_grads)
     pair_low = (
-        scatter_rows(jnp.stack(pair_grads), "ctx")
-        .astype(jnp.bfloat16)
-        .reshape(total_rows, 2 * columns)
+        scatter_rows(pair_terms, "ctx").astype(jnp.bfloat16).reshape(total_rows, 2 * columns)
     )
     stacked = jnp.stack([query_grad_low, pair_low[:, :columns], pair_low[:, columns:]])
     branch_low, stacked = lax.optimization_barrier((branch_low, stacked))
@@ -279,18 +412,21 @@
         [norm_sums, out_bias_grad, proj_bias_grad, fc_bias_grad, qv_bias_grad[0], qv_bias_grad[1]]
     )
     packed = sum_all(sum_all(packed, "fsdp"), "ctx")
+    result = (
+        (middle + (branch_low.astype(jnp.float32) + proj_bias))
+        .astype(jnp.bfloat16)
+        .reshape(seq_count, seq_rows, model_width)
+    )
+    act_one_grad, packed, shard_qkv, shard_out = lax.optimization_barrier(
+        (act_one_grad, packed, shard_qkv, shard_out)
+    )
+    tokens_grad = (middle_grad + norm_back(act_one_grad, ln1_gain, normed_one, scale_one)).reshape(
+        seq_count, seq_rows, model_width
+    )
     hidden_here = fc_bias_grad.shape[0]
     norm_sums = packed[: 6 * model_width].reshape(6, model_width)
     fc_bias_sum = packed[6 * model_width : 6 * model_width + hidden_here]
     qv_sum = packed[6 * model_width + hidden_here :].reshape(2, columns)
-    result = (
-        (middle + (branch_low.astype(jnp.float32) + proj_bias))
-        .astype(jnp.bfloat16)
-        .reshape(seq_count, seq_rows, model_width)
-    )
-    tokens_grad = (middle_grad + norm_back(act_one_grad, ln1_gain, normed_one, scale_one)).reshape(
-        seq_count, seq_rows, model_width
-    )
     return (
         result,
         tokens_grad,

time: 464 us -> 427 us (0.920)
  matrix products: 78.5 us -> 32.3 us
  local copies, waits for them, and re-layouts: 84.2 us -> 39.5 us
  waiting for transfers between devices: 182 us -> 226 us
  Pallas kernels: 0 us -> 28.8 us
  other arithmetic: 55.7 us -> 43.1 us
    dot_general x42 -> x0, matrix products: 41.1 us -> none  [the longest x6 8.96 us: one_head(): jnp.einsum('qd,kd->qk', grad_head, value_head, preferred_element_type=jnp...]
    pallas_call x0 -> x2, Pallas kernels: none -> 28.8 us  [the longest x1 21.4 us: attend_back(): pl.pallas_call(attend_back_kernel, grid=(count,), in_specs=[pl.BlockSpec(...]
    all_gather x1, waiting for transfers between devices: 0.01 us -> 21.6 us  [body(): all_out = lax.all_gather(whole_out, 'tp', axis=0, tiled=True)]
    all_gather x2 -> x1, waiting for transfers between devices: 22.6 us -> 2.49 us  [body(): lax.all_gather(jnp.concatenate([fc_weight, proj_weight.T, out_weight.T],...]
    psum x1, waiting for transfers between devices: 0.01 us -> 19.8 us  [body(): branch_low = lax.psum(branch_part, 'tp')]
    while x38 -> x0, local copies, waits for them, and re-layouts: 10.3 us -> none  [the longest x2 6.17 us: query_side(): lax.fori_loop(0, heads_here, one_head, (query_grad, pair_term, delta_cols))]
    ppermute x18, waiting for transfers between devices: 23.5 us -> 31.9 us  [swap(): return lax.ppermute(values, axis_name, [(i, i ^ bit) for i in range(count)])]
    dynamic_update_slice x6 -> x0, local copies, waits for them, and re-layouts: 7.95 us -> none  [forward_item(): lax.dynamic_update_slice(log_sums, (row_top + jnp.log(row_total))[None],...]
  transfers between devices with their start and end apart: 26 -> 25, of which waited for: 12 -> 13; matrix products, arithmetic and copies ran while one was open for 43% -> 20% of each run, Pallas kernels for 0% -> 7%
where the time goes in v2:
time: 427 us; the launch traced here: 420 us
  waiting for transfers between devices  226 us (53%)
  other arithmetic  43.1 us (10%)
  local copies, waits for them, and re-layouts  39.5 us (9%)
  matrix products  32.3 us (8%)
  Pallas kernels  28.8 us (7%)
  starting transfers between devices  18 us (4%)
  blocking collectives  16.4 us (4%)
  between operations  15.3 us (4%)
    psum x1, waiting for transfers between devices, body(): lax.psum(act_two_part.astype(jnp.bfloat16), 'tp').astype(jnp.float32)  45.6 us
    psum x1, waiting for transfers between devices, body(): lax.psum(act_one_part.astype(jnp.bfloat16), 'tp').astype(jnp.float32)  39.2 us
    all_gather x1, waiting for transfers between devices, body(): all_mixed = lax.all_gather(mixed_flip, 'tp', axis=0, tiled=True)  38.3 us
    ppermute x18, waiting for transfers between devices, swap(): return lax.ppermute(values, axis_name, [(i, i ^ bit) for i in range(count)])  31.9 us
    all_gather x1, waiting for transfers between devices, body(): pair_whole = lax.all_gather(key_value, 'ctx', axis=1, tiled=True)  27.5 us
    all_gather x1, waiting for transfers between devices, body(): all_out = lax.all_gather(whole_out, 'tp', axis=0, tiled=True)  21.6 us
    pallas_call x1, Pallas kernels, attend_back(): pl.pallas_call(attend_back_kernel, grid=(count,), in_specs=[pl.BlockSpec(...  21.4 us
    psum x1, waiting for transfers between devices, body(): branch_low = lax.psum(branch_part, 'tp')  19.8 us
  transfers between devices with their start and end apart: 25, of which 13 were waited for; matrix products, arithmetic and copies ran while one was open for 20% of the time, Pallas kernels for 7%

profile of v2, /device:TPU:0, one launch (start us, length us, event | category | flops | bytes accessed | tf_op | source)
XLA Modules:
  0.0 419.7 jit_solution(9310278214827549550)
XLA Ops:
  8.4 2.0 pad_maximum_fusion.2
  11.6 16.4 %all_gather.16 = bf16[3,768,192]{2,0,1:T(4,128)(2,1)S(1)} all-gather(bf16[3,192,192]{2,0,1:T(4,128)(2,1)S(1)} %copy.101), channel_id=1, replica_groups=mesh['fsdp'=4,'ctx'=2,'tp'=4] {'fsdp'}, dimensions={1}, use_global_device_ids=true | all-gather | bytes 1105920 | tf_op jit(solution)/shard_map/all_gather | solution.py:264
  28.0 2.2 copy.102
  32.5 1.3 copy-done.13
  38.8 2.5 all-gather.5.cloned.1.call-done
  44.0 27.5 %all-gather.7.cloned.1.call-done.pair_ref = bf16[2,1024,384]{2,1,0:T(8,128)(2,1)} async-done(((bf16[2,512,384]{2,1,0:T(8,128)(2,1)}), bf16[2,1024,384]{2,1,0:T(8,128)(2,1)}) %all-gather.7.cloned.1.call-update) | async-done | bytes 1572880 | tf_op jit(solution)/shard_map/all_gather | solution.py:280
  71.5 1.4 copy-done
  72.9 7.4 %attend.1 = (bf16[192,1024]{1,0:T(8,128)(2,1)}, f32[2,3,512]{2,1,0:T(4,128)S(1)}) custom-call(bf16[2,512,192]{2,1,0:T(8,128)(2,1)S(1)} %bitcast.163, bf16[2,1024,384]{2,1,0:T(8,128)(2,1)S(1)} %copy-done, s32[1,512]{1,0:T(1,128)S(1)} %bitcast.167, s32[1024,1]{1,0:T(8,128)S(1)} %fusion.40.all_ref), custom_call_target="tpu_custom_call" | custom-call | flops 4026531840 | bytes 1966080 | tf_op jit(solution)/shard_map/attend/pallas_call | solution.py:100
  80.7 1.7 convert_reduce_fusion.2
  82.4 21.6 %all-gather.11.cloned.1.call-done = bf16[768,768]{1,0:T(8,128)(2,1)} async-done(((bf16[192,768]{1,0:T(8,128)(2,1)}), bf16[768,768]{1,0:T(8,128)(2,1)}) %all-gather.11.cloned.1.call-update) | async-done | bytes 1179664 | tf_op jit(solution)/shard_map/all_gather | solution.py:285
  104.0 38.3 %all-gather.9.cloned.1.call-done = bf16[768,1024]{1,0:T(8,128)(2,1)} async-done(((bf16[192,1024]{1,0:T(8,128)(2,1)}), bf16[768,1024]{1,0:T(8,128)(2,1)}) %all-gather.9.cloned.1.call-update) | async-done | bytes 1572880 | tf_op jit(solution)/shard_map/all_gather | solution.py:334
  142.2 3.4 fusion.65
  146.2 2.4 copy-done.22
  148.5 2.5 multiply_convert_fusion
  151.1 1.5 fusion.69
  152.6 1.5 copy-done.18
  154.9 4.9 %convert_reduce_fusion.1 = (f32[768]{0:T(1024)}, bf16[1024,768]{0,1:T(8,128)(2,1)S(1)}) fusion(f32[1024,768]{0,1:T(8,128)S(1)} %get-tuple-element.74, f32[768]{0:T(1024)S(1)} %copy-done.31, bf16[1024,768]{1,0:T(8,128)(2,1)S(1)} %bitcast.170, bf16[768,1728]{1,0:T(8,128)(2,1)S(1)} %copy-done.22), kind=kOutput, calls=%fused_computation.34 | convolution fusion | flops 1226046720 | bytes 7478272 | tf_op jit(solution)/shard_map/dot_general | solution.py:349
  159.9 1.8 fusion.67
  162.4 3.6 fusion.66
  166.1 1.7 bitcast_add_fusion.2
  167.8 1.5 collective-permute-start.16
  172.2 5.5 %collective-permute-done.16 = bf16[1,1,192,768]{3,2,1,0:T(8,128)(2,1)S(1)} collective-permute-done((bf16[1,1,192,768]{3,2,1,0:T(8,128)(2,1)S(1)}, bf16[1,1,192,768]{3,2,1,0:T(8,128)(2,1)S(1)}, u32[]{:S(2)}, u32[]{:S(2)}) %collective-permute-start.16) | collective-permute-done | bytes 294944 | tf_op jit(solution)/shard_map/ppermute | solution.py:33
  177.8 1.5 collective-permute-start.17
  179.4 3.9 convolution_convert_fusion
  183.2 1.8 fusion.46
  185.1 1.4 collective-permute-start.14
  186.5 1.9 add_bitcast_fusion
  188.3 45.6 %all-reduce.4.cloned.1.call-done = bf16[1024,768]{1,0:T(8,128)(2,1)} async-done(((bf16[1024,768]{1,0:T(8,128)(2,1)}), bf16[1024,768]{1,0:T(8,128)(2,1)}) %all-reduce.4.cloned.1.call-update) | async-done | bytes 1572880 | tf_op jit(solution)/shard_map/psum | solution.py:356
  234.0 1.8 convert_element_type.315
  236.3 3.1 multiply_reduce_fusion
  239.4 1.5 convert_reduce_fusion.3
  241.0 1.8 fusion.58
  242.8 1.7 convolution_convert_fusion.1
  246.6 1.4 copy-done.1
  248.0 21.4 %attend_back.1 = (bf16[2,512,192]{2,1,0:T(8,128)(2,1)S(1)}, f32[2,1024,384]{2,1,0:T(8,128)}) custom-call(bf16[2,512,192]{2,1,0:T(8,128)(2,1)S(1)} %bitcast.164, bf16[2,1024,384]{2,1,0:T(8,128)(2,1)S(1)} %copy-done.1, bf16[2,512,192]{2,1,0:T(8,128)(2,1)S(1)} %bitcast.166, f32[2,3,512]{2,1,0:T(4,128)S(1)} %get-tuple-element.33.lse_ref, ...), custom_call_target="tpu_custom_call" | custom-call | flops 10066329600 | bytes 3932160 | tf_op jit(solution)/shard_map/attend_back/pallas_call | solution.py:155
  269.4 2.4 fusion.35
  272.1 1.5 collective-permute-start
  274.7 1.5 collective-permute-start.10
  276.2 1.9 add_bitcast_fusion.1
  278.3 1.3 collective-permute-done.10
  280.3 12.5 %collective-permute-done = bf16[2,1,512,384]{3,2,0,1:T(8,128)(2,1)S(1)} collective-permute-done((bf16[2,1,512,384]{3,2,0,1:T(8,128)(2,1)}, bf16[2,1,512,384]{3,2,0,1:T(8,128)(2,1)S(1)}, u32[]{:S(2)}, u32[]{:S(2)}) %collective-permute-start) | collective-permute-done | bytes 786464 | tf_op jit(solution)/shard_map/ppermute | solution.py:33
  292.8 1.6 fusion.25
  295.2 19.8 %all-reduce.6.cloned.1.call-done = bf16[1024,768]{1,0:T(8,128)(2,1)} async-done(((bf16[1024,768]{1,0:T(8,128)(2,1)}), bf16[1024,768]{1,0:T(8,128)(2,1)}) %all-reduce.6.cloned.1.call-update) | async-done | bytes 1572880 | tf_op jit(solution)/shard_map/psum | solution.py:358
  315.0 2.6 fusion.26
  317.5 3.6 bitcast_convert_fusion
  321.2 3.6 reshape_reshape.7
  324.8 2.7 fusion.7
  329.5 1.7 copy.123
  331.3 1.6 collective-permute-start.2
  332.9 1.3 convert_reduce_fusion.4
  334.3 1.7 collective-permute-done.2
  336.1 2.8 constant_dynamic-slice_fusion.3
  338.9 2.8 copy.113
  341.7 1.5 collective-permute-start.4
  343.2 1.5 bitcast_add_fusion.4
  345.8 1.6 add_bitcast_fusion.2
  347.4 1.5 collective-permute-start.5
  348.9 5.3 %collective-permute-done.7 = bf16[3,1,192,192]{3,2,0,1:T(8,128)(2,1)S(1)} collective-permute-done((bf16[3,1,192,192]{3,2,0,1:T(8,128)(2,1)S(1)}, bf16[3,1,192,192]{3,2,0,1:T(8,128)(2,1)S(1)}, u32[]{:S(2)}, u32[]{:S(2)}) %collective-permute-start.7) | collective-permute-done | bytes 221216 | tf_op jit(solution)/shard_map/ppermute | solution.py:33
  354.3 1.5 collective-permute-start.8
  355.8 1.6 add_convert_fusion
  357.4 5.5 %collective-permute-done.8 = bf16[3,192,192]{2,1,0:T(8,128)(2,1)S(1)} collective-permute-done((bf16[3,192,192]{2,1,0:T(8,128)(2,1)S(1)}, bf16[3,192,192]{2,1,0:T(8,128)(2,1)S(1)}, u32[]{:S(2)}, u32[]{:S(2)}) %collective-permute-start.8) | collective-permute-done | bytes 221216 | tf_op jit(solution)/shard_map/ppermute | solution.py:33
  363.8 39.2 %all-reduce.8.cloned.1.call-done = bf16[1024,768]{1,0:T(8,128)(2,1)} async-done(((bf16[1024,768]{1,0:T(8,128)(2,1)}), bf16[1024,768]{1,0:T(8,128)(2,1)}) %all-reduce.8.cloned.1.call-update) | async-done | bytes 1572880 | tf_op jit(solution)/shard_map/psum | solution.py:406
  402.9 1.6 convert_element_type.329
  408.0 4.5 %fusion.22 = f32[1024,768]{1,0:T(8,128)} fusion(f32[1024,768]{1,0:T(8,128)} %copy-done.7, bf16[2,512,768]{2,1,0:T(8,128)(2,1)S(1)} %copy-done.3, f32[1024,768]{1,0:T(8,128)} %copy-done.8, f32[1024]{0:T(1024)S(1)} %broadcast_multiply_fusion, f32[1024]{0:T(1024)S(1)} %broadcast_multiply_fusion.1, f32[768]{0:T(1024)S(1)} %copy-done.23, f32[1024]{0:T(1024)S(1)} %bitcast.194, ...), kind=kLoop, calls=%fused_computation.33 | loop fusion | flops 7077888 | bytes 11029504 | tf_op jit(solution)/shard_map/add | solution.py:423
  (167 shorter events, 30.9 us)
Async XLA Ops:
  7.2 3.2 copy-start.2
  7.2 4.2 copy-start.21
  7.2 34.1 %all-gather.5.cloned.1.call-start = ((), (), s32[]{:S(2)}) async-start(), calls=%async_computation | async-start | bytes 3440640 | tf_op jit(solution)/shard_map/all_gather | solution.py:266
  10.3 61.2 %all-gather.7.cloned.1.call-start = ((), (), s32[]{:S(2)}) async-start(), calls=%async_computation.1 | async-start | bytes 2359296 | tf_op jit(solution)/shard_map/all_gather | solution.py:280
  10.7 19.5 %copy-start.23 = (f32[768]{0:T(1024)S(1)}, f32[768]{0:T(1024)}, u32[]{:S(2)}) copy-start(f32[768]{0:T(1024)} %param.16) | copy-start | bytes 9220
  10.7 19.4 %copy-start.25 = (f32[768]{0:T(1024)S(1)}, f32[768]{0:T(1024)}, u32[]{:S(2)}) copy-start(f32[768]{0:T(1024)} %param.17) | copy-start | bytes 9220
  30.1 1.2 copy-start.19
  30.8 1.6 copy-start.14
  32.4 1.4 copy-start.13
  32.5 3.7 copy-start.28
  36.3 7.0 %copy-start.29 = (s32[4]{0:T(128)S(1)}, s32[4]{0:T(128)}, u32[]{:S(2)}) copy-start(s32[4]{0:T(128)} %param.28) | copy-start | bytes 52
  37.5 66.4 %all-gather.11.cloned.1.call-start = ((), (), s32[]{:S(2)}) async-start(), calls=%async_computation.3 | async-start | bytes 1474560 | tf_op jit(solution)/shard_map/all_gather | solution.py:285
  43.3 99.0 %all-gather.9.cloned.1.call-start = ((), (), s32[]{:S(2)}) async-start(), calls=%async_computation.2 | async-start | bytes 1966080 | tf_op jit(solution)/shard_map/all_gather | solution.py:334
  71.5 1.4 copy-start
  72.9 69.3 %copy-start.30 = (f32[768]{0:T(1024)S(1)}, f32[768]{0:T(1024)}, u32[]{:S(2)}) copy-start(f32[768]{0:T(1024)} %param.21) | copy-start | bytes 9220
  80.3 153.6 %all-reduce.4.cloned.1.call-start = ((), (), s32[]{:S(2)}) async-start(), calls=%async_computation.4 | async-start | bytes 3145728 | tf_op jit(solution)/shard_map/psum | solution.py:356
  145.6 14.3 %copy-start.4 = (f32[1024,768]{1,0:T(8,128)}, f32[1024,768]{1,0:T(8,128)S(1)}, u32[]{:S(2)}) copy-start(f32[1024,768]{1,0:T(8,128)S(1)} %get-tuple-element.70) | copy-start | bytes 9437188
  145.6 2.9 copy-start.22
  145.6 2.9 copy-start.24
  145.6 2.9 copy-start.31
  145.6 2.9 copy-start.32
  148.5 2.6 copy-start.10
  151.1 1.5 copy-start.33
  152.6 1.5 copy-start.18
  154.9 11.1 %collective-permute-start.15 = (bf16[1,2,192,768]{3,2,1,0:T(8,128)(2,1)}, bf16[1,2,192,768]{3,2,1,0:T(8,128)(2,1)}, u32[]{:S(2)}, u32[]{:S(2)}) collective-permute-start(bf16[1,2,192,768]{3,2,1,0:T(8,128)(2,1)} %fusion.39), channel_id=1, source_target_pairs={{0,8},{8,0},{16,24},{24,16},{1,9},{9,1},{17,25},{25,17},{2,10},{10... | collective-permute-start | bytes 1769480 | tf_op jit(solution)/shard_map/ppermute | solution.py:33
  161.7 4.2 %copy-start.16 = (f32[768,768]{1,0:T(8,128)}, f32[768,768]{1,0:T(8,128)S(1)}, u32[]{:S(2)}) copy-start(f32[768,768]{1,0:T(8,128)S(1)} %fusion.67) | copy-start | bytes 7077892
  161.8 7.6 %collective-permute-start.12 = (bf16[1,2,192,768]{3,2,1,0:T(8,128)(2,1)S(1)}, bf16[1,2,192,768]{3,2,1,0:T(8,128)(2,1)}, u32[]{:S(2)}, u32[]{:S(2)}) collective-permute-start(bf16[1,2,192,768]{3,2,1,0:T(8,128)(2,1)S(1)} %fusion.38), channel_id=1, source_target_pairs={{0,8},{8,0},{16,24},{24,16},{1,9},{9,1},{17,25},{25,17},{2,10},{10... | collective-permute-start | bytes 1769480 | tf_op jit(solution)/shard_map/ppermute | solution.py:33
  166.0 149.0 %all-reduce.6.cloned.1.call-start = ((), (), s32[]{:S(2)}) async-start(), calls=%async_computation.5 | async-start | bytes 3145728 | tf_op jit(solution)/shard_map/psum | solution.py:358
  166.0 3.3 copy-start.17
  167.8 11.6 %copy-start.34 = (bf16[1024,768]{0,1:T(8,128)(2,1)S(1)}, bf16[1024,768]{0,1:T(8,128)(2,1)}, u32[]{:S(2)}) copy-start(bf16[1024,768]{0,1:T(8,128)(2,1)} %copy-done.33) | copy-start | bytes 4718596
  167.8 9.9 %collective-permute-start.16 = (bf16[1,1,192,768]{3,2,1,0:T(8,128)(2,1)S(1)}, bf16[1,1,192,768]{3,2,1,0:T(8,128)(2,1)S(1)}, u32[]{:S(2)}, u32[]{:S(2)}) collective-permute-start(bf16[1,1,192,768]{3,2,1,0:T(8,128)(2,1)S(1)} %dynamic-slice_convert_fusion.1), channel_id=1, source_target_pairs={{0,16},{8,24},{16,0},{24,8},{1,17},{9,25},{17,1},{25,9},{2,18},{10... | collective-permute-start | bytes 884744 | tf_op jit(solution)/shard_map/ppermute | solution.py:33
  170.6 1.0 copy-start.11
  171.7 11.6 %collective-permute-start.13 = (bf16[1,1,192,768]{3,2,1,0:T(8,128)(2,1)S(1)}, bf16[1,1,192,768]{3,2,1,0:T(8,128)(2,1)S(1)}, u32[]{:S(2)}, u32[]{:S(2)}) collective-permute-start(bf16[1,1,192,768]{3,2,1,0:T(8,128)(2,1)S(1)} %dynamic-slice_convert_fusion.2), channel_id=1, source_target_pairs={{0,16},{8,24},{16,0},{24,8},{1,17},{9,25},{17,1},{25,9},{2,18},{10... | collective-permute-start | bytes 884744 | tf_op jit(solution)/shard_map/ppermute | solution.py:33
  177.8 8.6 %collective-permute-start.17 = (bf16[1,192,768]{2,1,0:T(8,128)(2,1)S(1)}, bf16[1,192,768]{2,1,0:T(8,128)(2,1)}, u32[]{:S(2)}, u32[]{:S(2)}) collective-permute-start(bf16[1,192,768]{2,1,0:T(8,128)(2,1)S(1)} %fusion.47), channel_id=1, source_target_pairs={{0,4},{4,0},{1,5},{5,1},{2,6},{6,2},{3,7},{7,3},{8,12},{12,8},{9,1... | collective-permute-start | bytes 884744 | tf_op jit(solution)/shard_map/ppermute | solution.py:33
  185.1 91.1 %collective-permute-start.14 = (bf16[1,192,768]{2,1,0:T(8,128)(2,1)}, bf16[1,192,768]{2,1,0:T(8,128)(2,1)}, u32[]{:S(2)}, u32[]{:S(2)}) collective-permute-start(bf16[1,192,768]{2,1,0:T(8,128)(2,1)} %fusion.46), channel_id=1, source_target_pairs={{0,4},{4,0},{1,5},{5,1},{2,6},{6,2},{3,7},{7,3},{8,12},{12,8},{9,1... | collective-permute-start | bytes 884744 | tf_op jit(solution)/shard_map/ppermute | solution.py:33
  234.0 2.4 copy-start.5
  241.0 1.8 copy-start.7
  246.3 27.4 %collective-permute-start.9 = (bf16[1,2,192,192]{2,3,1,0:T(8,128)(2,1)}, bf16[1,2,192,192]{2,3,1,0:T(8,128)(2,1)}, u32[]{:S(2)}, u32[]{:S(2)}) collective-permute-start(bf16[1,2,192,192]{2,3,1,0:T(8,128)(2,1)} %bitcast.162), channel_id=1, source_target_pairs={{0,8},{8,0},{16,24},{24,16},{1,9},{9,1},{17,25},{25,17},{2,10},{10... | collective-permute-start | bytes 442376 | tf_op jit(solution)/shard_map/ppermute | solution.py:33
  246.5 156.4 %all-reduce.8.cloned.1.call-start = ((), (), s32[]{:S(2)}) async-start(), calls=%async_computation.6 | async-start | bytes 3145728 | tf_op jit(solution)/shard_map/psum | solution.py:406
  246.6 1.4 copy-start.1
  272.1 20.7 %collective-permute-start = (bf16[2,1,512,384]{3,2,0,1:T(8,128)(2,1)}, bf16[2,1,512,384]{3,2,0,1:T(8,128)(2,1)S(1)}, u32[]{:S(2)}, u32[]{:S(2)}) collective-permute-start(bf16[2,1,512,384]{3,2,0,1:T(8,128)(2,1)} %fusion.35), channel_id=1, source_target_pairs={{0,4},{4,0},{1,5},{5,1},{2,6},{6,2},{3,7},{7,3},{8,12},{12,8},{9,1... | collective-permute-start | bytes 2359304 | tf_op jit(solution)/shard_map/ppermute | solution.py:33
  274.7 5.0 %collective-permute-start.10 = (bf16[1,1,192,192]{2,3,1,0:T(8,128)(2,1)S(1)}, bf16[1,1,192,192]{2,3,1,0:T(8,128)(2,1)S(1)}, u32[]{:S(2)}, u32[]{:S(2)}) collective-permute-start(bf16[1,1,192,192]{2,3,1,0:T(8,128)(2,1)S(1)} %dynamic-slice_convert_fusion.4), channel_id=1, source_target_pairs={{0,16},{8,24},{16,0},{24,8},{1,17},{9,25},{17,1},{25,9},{2,18},{10... | collective-permute-start | bytes 221192 | tf_op jit(solution)/shard_map/ppermute | solution.py:33
  279.7 66.2 %collective-permute-start.11 = (bf16[1,192,192]{1,2,0:T(8,128)(2,1)S(1)}, bf16[1,192,192]{1,2,0:T(8,128)(2,1)}, u32[]{:S(2)}, u32[]{:S(2)}) collective-permute-start(bf16[1,192,192]{1,2,0:T(8,128)(2,1)S(1)} %fusion.49), channel_id=1, source_target_pairs={{0,4},{4,0},{1,5},{5,1},{2,6},{6,2},{3,7},{7,3},{8,12},{12,8},{9,1... | collective-permute-start | bytes 221192 | tf_op jit(solution)/shard_map/ppermute | solution.py:33
  295.2 22.3 %copy-start.12 = (bf16[3,1024,192]{1,2,0:T(8,128)(2,1)}, bf16[3,1024,192]{1,2,0:T(8,128)(2,1)S(1)}, u32[]{:S(2)}) copy-start(bf16[3,1024,192]{1,2,0:T(8,128)(2,1)S(1)} %pad_maximum_fusion) | copy-start | bytes 3538948
  315.0 2.6 copy-start.20
  321.2 3.6 copy-start.3
  324.8 3.7 copy-start.9
  327.5 8.5 %copy-start.26 = (f32[768]{0:T(1024)S(1)}, f32[768]{0:T(1024)}, u32[]{:S(2)}) copy-start(f32[768]{0:T(1024)} %get-tuple-element.77) | copy-start | bytes 9220
  327.5 3.8 collective-permute-start.1
  331.2 12.0 %collective-permute-start.6 = (bf16[3,2,192,192]{3,2,0,1:T(8,128)(2,1)S(1)}, bf16[3,2,192,192]{3,2,0,1:T(8,128)(2,1)}, u32[]{:S(2)}, u32[]{:S(2)}) collective-permute-start(bf16[3,2,192,192]{3,2,0,1:T(8,128)(2,1)S(1)} %bitcast.188), channel_id=1, source_target_pairs={{0,8},{8,0},{16,24},{24,16},{1,9},{9,1},{17,25},{25,17},{2,10},{10... | collective-permute-start | bytes 1327112 | tf_op jit(solution)/shard_map/ppermute | solution.py:33
  331.3 4.7 %collective-permute-start.2 = (f32[3072]{0:T(1024)S(1)}, f32[3072]{0:T(1024)S(1)}, u32[]{:S(2)}, u32[]{:S(2)}) collective-permute-start(f32[3072]{0:T(1024)S(1)} %fusion.84), channel_id=1, source_target_pairs={{0,2},{1,3},{2,0},{3,1},{4,6},{5,7},{6,4},{7,5},{8,10},{9,11},{10,... | collective-permute-start | bytes 36872 | tf_op jit(solution)/shard_map/ppermute | solution.py:33
  336.1 5.6 %collective-permute-start.3 = (f32[5760]{0:T(1024)S(1)}, f32[5760]{0:T(1024)S(1)}, u32[]{:S(2)}, u32[]{:S(2)}) collective-permute-start(f32[5760]{0:T(1024)S(1)} %concatenate.16), channel_id=1, source_target_pairs={{0,8},{8,0},{16,24},{24,16},{1,9},{9,1},{17,25},{25,17},{2,10},{10... | collective-permute-start | bytes 69128 | tf_op jit(solution)/shard_map/ppermute | solution.py:33
  341.7 14.2 %copy-start.6 = (f32[1024,768]{1,0:T(8,128)S(1)}, f32[1024,768]{1,0:T(8,128)}, u32[]{:S(2)}) copy-start(f32[1024,768]{1,0:T(8,128)} %copy-done.4) | copy-start | bytes 9437188
  341.7 14.1 %copy-start.15 = (bf16[1024,768]{1,0:T(8,128)(2,1)S(1)}, bf16[1024,768]{1,0:T(8,128)(2,1)}, u32[]{:S(2)}) copy-start(bf16[1024,768]{1,0:T(8,128)(2,1)} %all-reduce.6.cloned.1.call-done) | copy-start | bytes 4718596
  341.7 14.1 %copy-start.27 = (f32[768]{0:T(1024)S(1)}, f32[768]{0:T(1024)}, u32[]{:S(2)}) copy-start(f32[768]{0:T(1024)} %param.27) | copy-start | bytes 9220
  341.7 5.7 %collective-permute-start.4 = (f32[5760]{0:T(1024)S(1)}, f32[5760]{0:T(1024)S(1)}, u32[]{:S(2)}, u32[]{:S(2)}) collective-permute-start(f32[5760]{0:T(1024)S(1)} %add.286), channel_id=1, source_target_pairs={{0,16},{8,24},{16,0},{24,8},{1,17},{9,25},{17,1},{25,9},{2,18},{10... | collective-permute-start | bytes 69128 | tf_op jit(solution)/shard_map/ppermute | solution.py:33
  344.8 9.4 %collective-permute-start.7 = (bf16[3,1,192,192]{3,2,0,1:T(8,128)(2,1)S(1)}, bf16[3,1,192,192]{3,2,0,1:T(8,128)(2,1)S(1)}, u32[]{:S(2)}, u32[]{:S(2)}) collective-permute-start(bf16[3,1,192,192]{3,2,0,1:T(8,128)(2,1)S(1)} %dynamic-slice_convert_fusion.3), channel_id=1, source_target_pairs={{0,16},{8,24},{16,0},{24,8},{1,17},{9,25},{17,1},{25,9},{2,18},{10... | collective-permute-start | bytes 663560 | tf_op jit(solution)/shard_map/ppermute | solution.py:33
  347.4 10.0 %collective-permute-start.5 = (f32[5760]{0:T(1024)S(1)}, f32[5760]{0:T(1024)S(1)}, u32[]{:S(2)}, u32[]{:S(2)}) collective-permute-start(f32[5760]{0:T(1024)S(1)} %add.287), channel_id=1, source_target_pairs={{0,4},{4,0},{1,5},{5,1},{2,6},{6,2},{3,7},{7,3},{8,12},{12,8},{9,1... | collective-permute-start | bytes 69128 | tf_op jit(solution)/shard_map/ppermute | solution.py:33
  354.3 8.6 %collective-permute-start.8 = (bf16[3,192,192]{2,1,0:T(8,128)(2,1)S(1)}, bf16[3,192,192]{2,1,0:T(8,128)(2,1)S(1)}, u32[]{:S(2)}, u32[]{:S(2)}) collective-permute-start(bf16[3,192,192]{2,1,0:T(8,128)(2,1)S(1)} %fusion.45), channel_id=1, source_target_pairs={{0,4},{4,0},{1,5},{5,1},{2,6},{6,2},{3,7},{7,3},{8,12},{12,8},{9,1... | collective-permute-start | bytes 663560 | tf_op jit(solution)/shard_map/ppermute | solution.py:33
  404.6 1.7 copy-start.8
Sparse Core Ops, SparseCore 0:
  10.5 30.8 all-gather.4
  43.4 28.0 all-gather.6
  73.7 30.2 all-gather.10
  106.0 36.2 all-gather.8
  166.1 67.8 all-reduce.3
  246.6 68.2 all-reduce.5
  334.4 68.4 all-reduce.7
